TPU v7x, 256 devices: a whole 4x4x8 slice. The times are simulated.
256 devices in a mesh: seq: 32 (over x_hi, z, core), tp: 8 (over y, x_lo).
Axes of the slice: x: 4 (x_hi: 2, x_lo: 2; x = x_hi * 2 + x_lo), y: 4, z: 8, core: 2. Of those that a mesh axis runs over, the one named last changes fastest.
Arguments:
- queries: bfloat16 [8, 4096, 4096], P('tp', 'seq'), may hold values from -9 to 9
- key_rows: bfloat16 [8, 4096, 4096], P('tp', 'seq'), may hold values from -6 to 6
- values: bfloat16 [8, 4096, 4096], P('tp', 'seq'), may hold values from -6 to 6
- upstream: bfloat16 [8, 4096, 4096], P(None, 'seq', 'tp'), may hold values from -6 to 6
- out_weight: bfloat16 [4096, 4096], P(None, 'tp'), may hold values from -0.09375 to 0.09375
- blocks: int32 [64, 4], replicated, may hold values from 0 to 63, as said below
Outputs:
- attended: bfloat16 [8, 4096, 4096], P('tp', 'seq')
- grad_queries: bfloat16 [8, 4096, 4096], P('tp', 'seq')
- grad_keys: bfloat16 [8, 4096, 4096], P('tp', 'seq')
- grad_values: bfloat16 [8, 4096, 4096], P('tp', 'seq')
- grad_weight: float32 [4096, 4096], P('seq', 'tp')
Inputs may be any that keep to these rules, and one draw needn't show every extreme that they name: Row a lists the blocks a - 1, a and a + 1 modulo 64, then one block 2 to 62 blocks after a modulo 64; no row names a block twice.
All inputs are finite; a program needn't handle non-finite values.
Results may differ from a plain program's by a relative error of at most 0.022.
Values may be sent and summed in bfloat16 or wider, within the bound.
A program may use at most 128 MiB of HBM per device.

v0:
```python
import math

import jax
import jax.numpy as jnp
from jax import lax
from jax.sharding import PartitionSpec as P

HD = 128
BLK = 64
NB = 4


def forward_head(query_rows, key_rows, value_rows, blocks):
    block_count = blocks.shape[0]
    factor = 1.0 / math.sqrt(HD)
    query_tiles = query_rows.reshape(block_count, BLK, HD)
    key_set = key_rows.reshape(block_count, BLK, HD)[blocks].reshape(block_count, NB * BLK, HD)
    value_set = value_rows.reshape(block_count, BLK, HD)[blocks].reshape(block_count, NB * BLK, HD)
    scores = (
        jnp.einsum("qid,qjd->qij", query_tiles, key_set, preferred_element_type=jnp.float32)
        * factor
    )
    row_max = jnp.max(scores, axis=-1, keepdims=True)
    shifted = jnp.exp(scores - row_max)
    soft_probs = shifted / jnp.sum(shifted, axis=-1, keepdims=True)
    probs_low = soft_probs.astype(jnp.bfloat16)
    context = jnp.einsum(
        "qij,qjd->qid", probs_low, value_set, preferred_element_type=jnp.float32
    ).astype(jnp.bfloat16)
    return (context, soft_probs, probs_low, key_set, value_set)


def backward_head(query_rows, grad_rows, blocks, saved):
    context, soft_probs, probs_low, key_set, value_set = saved
    block_count = blocks.shape[0]
    factor = 1.0 / math.sqrt(HD)
    query_tiles = query_rows.reshape(block_count, BLK, HD)
    grad_tiles = grad_rows.reshape(block_count, BLK, HD)
    row_delta = jnp.sum(
        grad_tiles.astype(jnp.float32) * context.astype(jnp.float32), axis=-1, keepdims=True
    )
    dprobs = jnp.einsum("qid,qjd->qij", grad_tiles, value_set, preferred_element_type=jnp.float32)
    dscores = (soft_probs * (dprobs - row_delta) * factor).astype(jnp.bfloat16)
    query_grad = jnp.einsum(
        "qij,qjd->qid", dscores, key_set, preferred_element_type=jnp.float32
    ).astype(jnp.bfloat16)
    flat_list = blocks.reshape(-1)
    key_parts = jnp.einsum(
        "qij,qid->qjd", dscores, query_tiles, preferred_element_type=jnp.float32
    ).reshape(block_count * NB, BLK, HD)
    value_parts = jnp.einsum(
        "qij,qid->qjd", probs_low, grad_tiles, preferred_element_type=jnp.float32
    ).reshape(block_count * NB, BLK, HD)
    key_grad = (
        jnp.zeros((block_count, BLK, HD), jnp.float32)
        .at[flat_list]
        .add(key_parts)
        .astype(jnp.bfloat16)
    )
    value_grad = (
        jnp.zeros((block_count, BLK, HD), jnp.float32)
        .at[flat_list]
        .add(value_parts)
        .astype(jnp.bfloat16)
    )
    return (query_grad, key_grad, value_grad)


def on_device(queries, key_rows, values, upstream, out_weight, blocks):
    head_queries, head_keys, head_values = (
        lax.all_to_all(queries, "seq", split_axis=2, concat_axis=1, tiled=True),
        lax.all_to_all(key_rows, "seq", split_axis=2, concat_axis=1, tiled=True),
        lax.all_to_all(values, "seq", split_axis=2, concat_axis=1, tiled=True),
    )
    length = head_queries.shape[1]
    count_heads = head_queries.shape[2] // HD

    def split_heads(array):
        return array.reshape(length, count_heads, HD).transpose(1, 0, 2)

    def join_heads(array):
        return (
            array.reshape(count_heads, length, HD)
            .transpose(1, 0, 2)
            .reshape(1, length, count_heads * HD)
        )

    grad_tokens = lax.psum_scatter(
        jnp.einsum("stc,dc->std", upstream, out_weight, preferred_element_type=jnp.float32).astype(
            jnp.bfloat16
        ),
        "tp",
        scatter_dimension=0,
        tiled=True,
    )
    grad_heads = lax.all_to_all(grad_tokens, "seq", split_axis=2, concat_axis=1, tiled=True)
    stacked = (
        split_heads(head_queries),
        split_heads(head_keys),
        split_heads(head_values),
        split_heads(grad_heads),
    )

    def both_one(packed):
        saved_one = forward_head(packed[0], packed[1], packed[2], blocks)
        return (saved_one[0],) + backward_head(packed[0], packed[3], blocks, saved_one)

    results = lax.map(both_one, stacked)
    attended, query_grad, key_grad, value_grad = (
        lax.all_to_all(join_heads(results[0]), "seq", split_axis=1, concat_axis=2, tiled=True),
        lax.all_to_all(join_heads(results[1]), "seq", split_axis=1, concat_axis=2, tiled=True),
        lax.all_to_all(join_heads(results[2]), "seq", split_axis=1, concat_axis=2, tiled=True),
        lax.all_to_all(join_heads(results[3]), "seq", split_axis=1, concat_axis=2, tiled=True),
    )
    every_sequence = lax.all_gather(attended, "tp", axis=0, tiled=True)
    grad_weight = lax.psum_scatter(
        jnp.einsum(
            "str,stc->rc", every_sequence, upstream, preferred_element_type=jnp.float32
        ).astype(jnp.bfloat16),
        "seq",
        scatter_dimension=0,
        tiled=True,
    ).astype(jnp.float32)
    return (attended, query_grad, key_grad, value_grad, grad_weight)


def solution(mesh):
    in_specs = (
        P("tp", "seq", None),
        P("tp", "seq", None),
        P("tp", "seq", None),
        P(None, "seq", "tp"),
        P(None, "tp"),
        P(),
    )
    out_specs = (
        P("tp", "seq", None),
        P("tp", "seq", None),
        P("tp", "seq", None),
        P("tp", "seq", None),
        P("seq", "tp"),
    )
    return jax.shard_map(
        on_device, mesh=mesh, in_specs=in_specs, out_specs=out_specs, check_vma=False
    )
```

profile of v0, /device:TPU:32, one launch (start us, length us, event | category | flops | bytes accessed | tf_op | source)
XLA Modules:
  0.0 870.8 jit_solution(8195947875667358401)
XLA Ops:
  8.4 8.9 %convolution_convert_fusion = bf16[8,128,4096]{2,1,0:T(8,128)(2,1)} fusion(bf16[8,128,512]{2,1,0:T(8,128)(2,1)S(1)} %copy-done, bf16[4096,512]{1,0:T(8,128)(2,1)} %param.10), kind=kOutput, calls=%fused_computation.6 | convolution fusion | flops 4299161600 | bytes 13631488 | tf_op jit(solution)/shard_map/stc,dc->std/dot_general | solution.py:89
  22.9 23.4 %reduce.1 = bf16[4096,128]{1,0:T(8,128)(2,1)} reduce(bf16[4096,1,128]{2,1,0:T(2,128)(2,1)S(1)} %bitcast.130, bf16[]{:T(256)} %broadcast.81), dimensions={1}, to_apply=%bitcast.71.reduce_sub_computation | reduce | bytes 2097154
  48.4 11.6 %all-to-all-start.2 = ((bf16[32,2,8192]{2,1,0:T(2,128)(2,1)}), bf16[32,2,8192]{2,1,0:T(2,128)(2,1)}, u32[]{:S(2)}, u32[]{:S(2)}) async-start(bf16[32,2,8192]{2,1,0:T(2,128)(2,1)} %reshape.139), calls=%async_computation.2 | async-start | bytes 2097152 | tf_op jit(solution)/shard_map/all_to_all | solution.py:73
  65.1 23.4 %reduce.2 = bf16[4096,128]{1,0:T(8,128)(2,1)} reduce(bf16[4096,1,128]{2,1,0:T(2,128)(2,1)S(1)} %bitcast.136, bf16[]{:T(256)} %broadcast.81), dimensions={1}, to_apply=%bitcast.73.reduce_sub_computation | reduce | bytes 2097154
  90.6 9.9 %all-to-all-start = ((bf16[32,2,8192]{2,1,0:T(2,128)(2,1)}), bf16[32,2,8192]{2,1,0:T(2,128)(2,1)}, u32[]{:S(2)}, u32[]{:S(2)}) async-start(bf16[32,2,8192]{2,1,0:T(2,128)(2,1)} %reshape.141), calls=%async_computation | async-start | bytes 2097152 | tf_op jit(solution)/shard_map/all_to_all | solution.py:72
  105.5 23.4 %reduce.3 = bf16[4096,128]{1,0:T(8,128)(2,1)} reduce(bf16[4096,1,128]{2,1,0:T(2,128)(2,1)S(1)} %bitcast.137, bf16[]{:T(256)} %broadcast.81), dimensions={1}, to_apply=%bitcast.75.reduce_sub_computation | reduce | bytes 2097154
  131.1 10.4 %all-to-all-start.1 = ((bf16[32,2,8192]{2,1,0:T(2,128)(2,1)}), bf16[32,2,8192]{2,1,0:T(2,128)(2,1)}, u32[]{:S(2)}, u32[]{:S(2)}) async-start(bf16[32,2,8192]{2,1,0:T(2,128)(2,1)} %reshape.143), calls=%async_computation.1 | async-start | bytes 2097152 | tf_op jit(solution)/shard_map/all_to_all | solution.py:71
  141.6 84.0 %reduce-scatter.3.cloned.1.call-done = bf16[1,128,4096]{2,1,0:T(8,128)(2,1)} async-done(((bf16[8,128,4096]{2,1,0:T(8,128)(2,1)}), bf16[1,128,4096]{2,1,0:T(8,128)(2,1)}) %reduce-scatter.3.cloned.1.call-update) | async-done | bytes 1048592 | tf_op jit(solution)/shard_map/reduce_scatter | solution.py:88
  230.6 23.4 %reduce = bf16[4096,128]{1,0:T(8,128)(2,1)} reduce(bf16[4096,1,128]{2,1,0:T(2,128)(2,1)S(1)} %bitcast.132, bf16[]{:T(256)} %broadcast.81), dimensions={1}, to_apply=%bitcast.79.reduce_sub_computation | reduce | bytes 2097154
  256.1 9.8 %all-to-all-start.4 = ((bf16[32,2,8192]{2,1,0:T(2,128)(2,1)}), bf16[32,2,8192]{2,1,0:T(2,128)(2,1)}, u32[]{:S(2)}, u32[]{:S(2)}) async-start(bf16[32,2,8192]{2,1,0:T(2,128)(2,1)} %reshape.147), calls=%async_computation.5 | async-start | bytes 2097152 | tf_op jit(solution)/shard_map/all_to_all | solution.py:96
  273.2 5.8 reshape.142
  313.8 12.7 %multiply_reduce_fusion = (f32[64,64]{1,0:T(8,128)S(1)}, bf16[64,64,128]{2,1,0:T(8,128)(2,1)S(1)}) fusion(bf16[64,64,128]{2,1,0:T(8,128)(2,1)} %bitcast.156, bf16[64,256,128]{2,1,0:T(8,128)(2,1)} %bitcast.149, f32[64,64]{1,0:T(8,128)S(1)} %get-tuple-element.65, f32[64,256,64]{1,2,0:T(8,128)} %copy-done.2), kind=kOutput, calls=%fused_computation.14 | convolution fusion | flops 276300032 | bytes 10518528 | tf_op jit(solution)/shard_map/while/body/eval_jaxpr/qij,qjd->qid/dot_general | solution.py:27
  326.6 17.2 %copy.116 = bf16[1,4096,128]{2,0,1:T(2,128)(2,1)} copy(bf16[1,4096,128]{2,1,0:T(8,128)(2,1)S(1)} %bitcast.155) | data formatting | bytes 2097152 | tf_op jit(solution)/shard_map/reshape;transpose;reshape | solution.py:85
  343.8 23.4 %reduce.4 = bf16[4096,128]{1,0:T(8,128)(2,1)S(1)} reduce(bf16[4096,1,128]{2,1,0:T(2,128)(2,1)} %bitcast.133, bf16[]{:T(256)} %broadcast.81), dimensions={1}, to_apply=%bitcast.113.reduce_sub_computation | reduce | bytes 2097154
  368.3 40.3 %all_to_all.132 = bf16[32,2,8192]{2,1,0:T(2,128)(2,1)S(1)} all-to-all(bf16[32,2,8192]{2,1,0:T(2,128)(2,1)} %reshape.145), channel_id=1, replica_groups=mesh['seq'=32,'tp'=8] {'seq'}, dimensions={0} | all-to-all | bytes 2097152 | tf_op jit(solution)/shard_map/all_to_all | solution.py:110
  417.5 7.5 multiply_convert_fusion
  425.0 158.5 %all-gather.2.cloned.1.call-done = bf16[8,128,4096]{2,1,0:T(8,128)(2,1)} async-done(((bf16[1,128,4096]{2,1,0:T(8,128)(2,1)}), bf16[8,128,4096]{2,1,0:T(8,128)(2,1)}) %all-gather.2.cloned.1.call-update) | async-done | bytes 8388624 | tf_op jit(solution)/shard_map/all_gather | solution.py:115
  583.5 9.7 %bitcast_convert_fusion = bf16[4096,512]{1,0:T(8,128)(2,1)} fusion(bf16[8,128,4096]{2,1,0:T(8,128)(2,1)} %all-gather.2.cloned.1.call-done, bf16[8,128,512]{2,1,0:T(8,128)(2,1)S(1)} %copy-done), kind=kOutput, calls=%fused_computation.5 | convolution fusion | flops 4297064448 | bytes 13631488 | tf_op jit(solution)/shard_map/str,stc->rc/dot_general | solution.py:117
  596.9 17.0 %copy.115 = bf16[1,4096,128]{2,0,1:T(2,128)(2,1)} copy(bf16[1,4096,128]{2,1,0:T(8,128)(2,1)S(1)} %bitcast.138) | data formatting | bytes 2097152 | tf_op jit(solution)/shard_map/reshape;transpose;reshape | solution.py:85
  614.0 23.5 %reduce.5 = bf16[4096,128]{1,0:T(8,128)(2,1)S(1)} reduce(bf16[4096,1,128]{2,1,0:T(2,128)(2,1)} %bitcast.134, bf16[]{:T(256)} %broadcast.81), dimensions={1}, to_apply=%bitcast.112.reduce_sub_computation | reduce | bytes 2097154
  638.5 10.4 %all-to-all-start.5 = ((bf16[32,2,8192]{2,1,0:T(2,128)(2,1)}), bf16[32,2,8192]{2,1,0:T(2,128)(2,1)}, u32[]{:S(2)}, u32[]{:S(2)}) async-start(bf16[32,2,8192]{2,1,0:T(2,128)(2,1)} %reshape.149), calls=%async_computation.6 | async-start | bytes 2097152 | tf_op jit(solution)/shard_map/all_to_all | solution.py:111
  649.1 6.1 fusion.25
  655.5 26.3 %scatter_fusion = f32[64,64,128]{2,1,0:T(8,128)S(1)} fusion(f32[64,64,128]{2,1,0:T(8,128)S(1)} %broadcast.50.clone, s32[256]{0:T(256)S(1)} %bitcast.159, f32[256,64,128]{2,1,0:T(8,128)} %bitcast.116), kind=kCustom, calls=%fused_computation.2 | custom fusion | flops 2097152 | bytes 25166848 | tf_op jit(solution)/shard_map/while/body/eval_jaxpr/scatter-add | solution.py:57
  682.0 16.7 %copy.114 = bf16[1,4096,128]{2,0,1:T(2,128)(2,1)S(1)} copy(bf16[1,4096,128]{2,1,0:T(8,128)(2,1)S(1)} %bitcast.139) | data formatting | bytes 2097152 | tf_op jit(solution)/shard_map/reshape;transpose;reshape | solution.py:85
  698.7 22.4 %reduce.6 = bf16[4096,128]{1,0:T(8,128)(2,1)S(1)} reduce(bf16[4096,1,128]{2,1,0:T(2,128)(2,1)S(1)} %bitcast.135, bf16[]{:T(256)} %broadcast.81), dimensions={1}, to_apply=%bitcast.111.reduce_sub_computation | reduce | bytes 2097154
  722.2 10.2 %all-to-all-start.6 = ((bf16[32,2,8192]{2,1,0:T(2,128)(2,1)}), bf16[32,2,8192]{2,1,0:T(2,128)(2,1)}, u32[]{:S(2)}, u32[]{:S(2)}) async-start(bf16[32,2,8192]{2,1,0:T(2,128)(2,1)} %reshape.151), calls=%async_computation.7 | async-start | bytes 2097152 | tf_op jit(solution)/shard_map/all_to_all | solution.py:112
  732.5 14.2 %fusion.10 = f32[64,256,128]{2,1,0:T(8,128)} fusion(bf16[64,64,128]{2,1,0:T(8,128)(2,1)S(1)} %bitcast.158, f32[64,64]{1,0:T(8,128)S(1)} %get-tuple-element.65, f32[64,256,64]{1,2,0:T(8,128)} %copy-done.2), kind=kOutput, calls=%fused_computation.24 | convolution fusion | flops 273682688 | bytes 13647872 | tf_op jit(solution)/shard_map/while/body/eval_jaxpr/qij,qid->qjd/dot_general | solution.py:51
  746.9 26.2 %scatter_fusion.1 = f32[64,64,128]{2,1,0:T(8,128)S(1)} fusion(f32[64,64,128]{2,1,0:T(8,128)S(1)} %broadcast.50.clone.1, s32[256]{0:T(256)S(1)} %bitcast.160, f32[256,64,128]{2,1,0:T(8,128)} %bitcast.129), kind=kCustom, calls=%fused_computation.3 | custom fusion | flops 2097152 | bytes 25166848 | tf_op jit(solution)/shard_map/while/body/eval_jaxpr/scatter-add | solution.py:63
  773.3 16.7 %copy.113 = bf16[1,4096,128]{2,0,1:T(2,128)(2,1)S(1)} copy(bf16[1,4096,128]{2,1,0:T(8,128)(2,1)S(1)} %bitcast.140) | data formatting | bytes 2097152 | tf_op jit(solution)/shard_map/reshape;transpose;reshape | solution.py:85
  790.1 22.4 %reduce.7 = bf16[4096,128]{1,0:T(8,128)(2,1)S(1)} reduce(bf16[4096,1,128]{2,1,0:T(2,128)(2,1)S(1)} %bitcast.131, bf16[]{:T(256)} %broadcast.81), dimensions={1}, to_apply=%bitcast.110.reduce_sub_computation | reduce | bytes 2097154
  813.6 9.9 %all-to-all-start.7 = ((bf16[32,2,8192]{2,1,0:T(2,128)(2,1)}), bf16[32,2,8192]{2,1,0:T(2,128)(2,1)}, u32[]{:S(2)}, u32[]{:S(2)}) async-start(bf16[32,2,8192]{2,1,0:T(2,128)(2,1)} %reshape.153), calls=%async_computation.8 | async-start | bytes 2097152 | tf_op jit(solution)/shard_map/all_to_all | solution.py:113
  836.3 17.7 %all-to-all-done.7 = bf16[32,2,8192]{2,1,0:T(2,128)(2,1)} async-done(((bf16[32,2,8192]{2,1,0:T(2,128)(2,1)}), bf16[32,2,8192]{2,1,0:T(2,128)(2,1)}, u32[]{:S(2)}, u32[]{:S(2)}) %all-to-all-start.7) | async-done | bytes 1048608 | tf_op jit(solution)/shard_map/all_to_all | solution.py:113
  (80 shorter events, 113.5 us)
Async XLA Ops:
  7.2 1.2 copy-start
  7.2 218.3 %reduce-scatter.3.cloned.1.call-start = ((), (), s32[]{:S(2)}) async-start(), calls=%async_computation.10 | async-start | bytes 9437184 | tf_op jit(solution)/shard_map/reduce_scatter | solution.py:88
  48.4 42.2 %all-to-all-start.2 = ((bf16[32,2,8192]{2,1,0:T(2,128)(2,1)}), bf16[32,2,8192]{2,1,0:T(2,128)(2,1)}, u32[]{:S(2)}, u32[]{:S(2)}) async-start(bf16[32,2,8192]{2,1,0:T(2,128)(2,1)} %reshape.139), calls=%async_computation.2 | async-start | bytes 2097152 | tf_op jit(solution)/shard_map/all_to_all | solution.py:73
  90.6 40.5 %all-to-all-start = ((bf16[32,2,8192]{2,1,0:T(2,128)(2,1)}), bf16[32,2,8192]{2,1,0:T(2,128)(2,1)}, u32[]{:S(2)}, u32[]{:S(2)}) async-start(bf16[32,2,8192]{2,1,0:T(2,128)(2,1)} %reshape.141), calls=%async_computation | async-start | bytes 2097152 | tf_op jit(solution)/shard_map/all_to_all | solution.py:72
  131.1 124.9 %all-to-all-start.1 = ((bf16[32,2,8192]{2,1,0:T(2,128)(2,1)}), bf16[32,2,8192]{2,1,0:T(2,128)(2,1)}, u32[]{:S(2)}, u32[]{:S(2)}) async-start(bf16[32,2,8192]{2,1,0:T(2,128)(2,1)} %reshape.143), calls=%async_computation.1 | async-start | bytes 2097152 | tf_op jit(solution)/shard_map/all_to_all | solution.py:71
  230.5 35.4 %copy-start.4 = (s32[64,4]{0,1:T(4,128)S(1)}, s32[64,4]{0,1:T(4,128)}, u32[]{:S(2)}) copy-start(s32[64,4]{0,1:T(4,128)} %param.11) | copy-start | bytes 3076
  256.1 49.0 %all-to-all-start.4 = ((bf16[32,2,8192]{2,1,0:T(2,128)(2,1)}), bf16[32,2,8192]{2,1,0:T(2,128)(2,1)}, u32[]{:S(2)}, u32[]{:S(2)}) async-start(bf16[32,2,8192]{2,1,0:T(2,128)(2,1)} %reshape.147), calls=%async_computation.5 | async-start | bytes 2097152 | tf_op jit(solution)/shard_map/all_to_all | solution.py:96
  265.9 317.6 %all-gather.2.cloned.1.call-start = ((), (), s32[]{:S(2)}) async-start(), calls=%async_computation.11 | async-start | bytes 9437184 | tf_op jit(solution)/shard_map/all_gather | solution.py:115
  300.2 2.0 copy-start.2
  417.4 445.0 %reduce-scatter.5.cloned.1.call-start = ((), (), s32[]{:S(2)}) async-start(), calls=%async_computation.12 | async-start | bytes 4325376 | tf_op jit(solution)/shard_map/reduce_scatter | solution.py:116
  638.5 83.7 %all-to-all-start.5 = ((bf16[32,2,8192]{2,1,0:T(2,128)(2,1)}), bf16[32,2,8192]{2,1,0:T(2,128)(2,1)}, u32[]{:S(2)}, u32[]{:S(2)}) async-start(bf16[32,2,8192]{2,1,0:T(2,128)(2,1)} %reshape.149), calls=%async_computation.6 | async-start | bytes 2097152 | tf_op jit(solution)/shard_map/all_to_all | solution.py:111
  721.1 11.4 %copy-start.3 = (bf16[1,32,128,128]{3,2,1,0:T(8,128)(2,1)S(1)}, bf16[1,32,128,128]{3,2,1,0:T(8,128)(2,1)}, u32[]{:S(2)}) copy-start(bf16[1,32,128,128]{3,2,1,0:T(8,128)(2,1)} %copy.86) | copy-start | bytes 3145732
  722.2 91.3 %all-to-all-start.6 = ((bf16[32,2,8192]{2,1,0:T(2,128)(2,1)}), bf16[32,2,8192]{2,1,0:T(2,128)(2,1)}, u32[]{:S(2)}, u32[]{:S(2)}) async-start(bf16[32,2,8192]{2,1,0:T(2,128)(2,1)} %reshape.151), calls=%async_computation.7 | async-start | bytes 2097152 | tf_op jit(solution)/shard_map/all_to_all | solution.py:112
  813.6 40.4 %all-to-all-start.7 = ((bf16[32,2,8192]{2,1,0:T(2,128)(2,1)}), bf16[32,2,8192]{2,1,0:T(2,128)(2,1)}, u32[]{:S(2)}, u32[]{:S(2)}) async-start(bf16[32,2,8192]{2,1,0:T(2,128)(2,1)} %reshape.153), calls=%async_computation.8 | async-start | bytes 2097152 | tf_op jit(solution)/shard_map/all_to_all | solution.py:113
  854.0 10.1 %copy-start.1 = (bf16[8,128,512]{2,1,0:T(8,128)(2,1)S(1)}, bf16[8,128,512]{2,1,0:T(8,128)(2,1)}, u32[]{:S(2)}) copy-start(bf16[8,128,512]{2,1,0:T(8,128)(2,1)} %param.9) | copy-start | bytes 3145732
Sparse Core Ops, SparseCore 0:
  17.5 208.0 reduce-scatter.2
  417.5 165.8 all-gather.1
  593.4 137.3 reduce-scatter.4
where the time goes:
time: 881 us; the launch traced here: 871 us
  waiting for transfers between devices  260 us (30%)
  other arithmetic  243 us (28%)
  local copies, waits for them, and re-layouts  174 us (20%)
  starting transfers between devices  72.4 us (8%)
  matrix products  66.6 us (8%)
  blocking collectives  40.3 us (5%)
  between operations  14.3 us (2%)
    unnamed x8, other arithmetic  185 us
    all_gather x1, waiting for transfers between devices, on_device(): every_sequence = lax.all_gather(attended, 'tp', axis=0, tiled=True)  159 us
    unnamed x43, local copies, waits for them, and re-layouts  84.4 us
    reduce_scatter x1, waiting for transfers between devices, on_device(): lax.psum_scatter(jnp.einsum('stc,dc->std', upstream, out_weight, preferre...  84 us
    another operation x4, local copies, waits for them, and re-layouts, join_heads(): return array.reshape(count_heads, length, HD).transpose(1, 0, 2).reshape(...  67.7 us
    all_to_all x1, blocking collectives, on_device(): lax.all_to_all(join_heads(results[0]), 'seq', split_axis=1, concat_axis=2...  40.3 us
    scatter-add x1, other arithmetic, backward_head(): key_grad = jnp.zeros((block_count, BLK, HD), jnp.float32).at[flat_list].a...  26.3 us
    scatter-add x1, other arithmetic, backward_head(): value_grad = jnp.zeros((block_count, BLK, HD), jnp.float32).at[flat_list]...  26.2 us
  transfers between devices with their start and end apart: 10, of which 4 were waited for; matrix products, arithmetic and copies ran while one was open for 45% of the time, Pallas kernels for 0%

commit v1 on v0

v1 whole, which is shorter than its diff:
```python
import functools
import math

import jax
import jax.numpy as jnp
from jax import lax
from jax.experimental import pallas as pl
from jax.experimental.pallas import tpu as pltpu
from jax.sharding import PartitionSpec as P

HD = 128
BLK = 64
NB = 4
MESH = pl.DeviceIdType.MESH
BF16 = jnp.bfloat16
F32 = jnp.float32

NZ = 8
NY = 4
NSEQ = 32
ROWS = 128
WIDE = 512
D = 4096


def seq_of(x_hi, z, core):
    return x_hi * 16 + z * 2 + core


def near_far(step, place, count):
    half = (step + 1) // 2
    return lax.rem(jnp.where(lax.rem(step, 2) == 1, place + half, place + count - half), count)


def seq_peer(step, me):
    z = near_far(step // 4, lax.rem(me // 2, NZ), NZ)
    x_hi = lax.rem(me // 16 + lax.rem(step, 2), 2)
    core = lax.rem(lax.rem(me, 2) + lax.rem(step // 2, 2), 2)
    return seq_of(x_hi, z, core)


def col(index):
    return pl.ds(pl.multiple_of(index * HD, HD), HD)


def row(index, size=ROWS):
    return pl.ds(pl.multiple_of(index * size, size), size)


def chunk_at(step, z):
    return near_far(NZ - 1 - step, z, NZ)


def enter(me, tp):
    barrier = pltpu.get_barrier_semaphore()

    def greet_seq(d, carry):
        pl.semaphore_signal(
            barrier, inc=1, device_id=(lax.rem(me + d, NSEQ), tp), device_id_type=MESH
        )
        return carry

    def greet_tp(d, carry):
        pl.semaphore_signal(
            barrier, inc=1, device_id=(me, lax.rem(tp + d, 8)), device_id_type=MESH
        )
        return carry

    lax.fori_loop(1, NSEQ, greet_seq, 0)
    lax.fori_loop(1, 8, greet_tp, 0)
    pl.semaphore_wait(barrier, NSEQ - 1 + 7)


def gather_in_kernel(
    q_ref, k_ref, v_ref, u_ref, w_ref,
    qh_ref, kh_ref, vh_ref, gh_ref,
    u_buf, w_buf, terms, y_got, keep, x_send, x_got, g_send,
    load_sem, own_sem, send_sem, recv_sem, y_send_sem, y_recv_sem, x_send_sem, x_recv_sem,
    g_send_sem, g_recv_sem, g_own_sem,
):
    me = lax.axis_index("seq")
    tp = lax.axis_index("tp")
    z = lax.rem(me // 2, NZ)
    y, x_lo = tp // 2, lax.rem(tp, 2)
    load_u = pltpu.make_async_copy(u_ref, u_buf, load_sem.at[0])
    load_w = pltpu.make_async_copy(w_ref, w_buf, load_sem.at[1])
    load_u.start()
    load_w.start()
    enter(me, tp)

    sources = (q_ref, k_ref, v_ref)
    targets = (qh_ref, kh_ref, vh_ref)
    for a in range(3):
        pltpu.make_async_copy(
            sources[a].at[:, col(me)], targets[a].at[row(me), :], own_sem.at[a]
        ).start()

        def send_heads(step, carry, a=a):
            peer = seq_peer(step, me)
            pltpu.make_async_remote_copy(
                src_ref=sources[a].at[:, col(peer)],
                dst_ref=targets[a].at[row(me), :],
                send_sem=send_sem.at[a],
                recv_sem=recv_sem.at[a],
                device_id=(peer, tp),
                device_id_type=MESH,
            ).start()
            return carry

        lax.fori_loop(1, NSEQ, send_heads, 0)

    load_u.wait()
    load_w.wait()

    def y_copy(j, d):
        other = lax.rem(y + d, NY)
        return pltpu.make_async_remote_copy(
            src_ref=terms.at[j, row(other, 256), :],
            dst_ref=y_got.at[j, d - 1],
            send_sem=y_send_sem.at[j, d - 1],
            recv_sem=y_recv_sem.at[j, d - 1],
            device_id=(me, other * 2 + x_lo),
            device_id_type=MESH,
        )

    def x_copy(j):
        return pltpu.make_async_remote_copy(
            src_ref=x_send.at[j],
            dst_ref=x_got.at[j],
            send_sem=x_send_sem.at[j],
            recv_sem=x_recv_sem.at[j],
            device_id=(me, y * 2 + 1 - x_lo),
            device_id_type=MESH,
        )

    def stage_terms(j):
        chunk = chunk_at(j, z)
        for part in range(2):
            rows = pl.ds(pl.multiple_of(part * 2048 + chunk * 256, 256), 256)
            terms[j, :, part * 256 : (part + 1) * 256] = lax.dot_general(
                u_buf[...], w_buf[rows, :], (((1,), (1,)), ((), ())), preferred_element_type=F32
            ).astype(BF16)
        for d in (2, 1, 3):
            y_copy(j, d).start()

    def stage_y(j):
        for d in (1, 2, 3):
            y_copy(j, d).wait_recv()

        def total(x):
            rows = pl.ds(pl.multiple_of(y * 256 + x * 128, 128), 128)
            here = pl.ds(pl.multiple_of(x * 128, 128), 128)
            result = terms[j, rows, :].astype(F32)
            for d in range(3):
                result = result + y_got[j, d, here, :].astype(F32)
            return result

        x_send[j] = total(1 - x_lo).astype(BF16)
        x_copy(j).start()
        keep[j] = total(x_lo)

    def stage_x(j):
        x_copy(j).wait_recv()
        g_send[j] = (keep[j] + x_got[j].astype(F32)).astype(BF16)
        chunk = chunk_at(j, z)
        for part in range(4):
            peer = seq_of(part // 2, chunk, part % 2)
            source = g_send.at[j, :, part * HD : (part + 1) * HD]
            target = gh_ref.at[row(me), :]

            @pl.when(peer == me)
            def _():
                pltpu.make_async_copy(source, target, g_own_sem).start()

            @pl.when(peer != me)
            def _():
                pltpu.make_async_remote_copy(
                    src_ref=source,
                    dst_ref=target,
                    send_sem=g_send_sem,
                    recv_sem=g_recv_sem,
                    device_id=(peer, tp),
                    device_id_type=MESH,
                ).start()

    def step(j, carry):
        @pl.when(j < 8)
        def _():
            stage_terms(j)

        @pl.when((j >= 2) & (j < 10))
        def _():
            stage_y(j - 2)

        @pl.when(j >= 3)
        def _():
            stage_x(j - 3)

        return carry

    lax.fori_loop(0, 11, step, 0)

    def drain(j, carry):
        for d in (1, 2, 3):
            y_copy(j, d).wait_send()
        x_copy(j).wait_send()
        return carry

    lax.fori_loop(0, 8, drain, 0)
    many = gh_ref.at[pl.ds(0, 31 * ROWS)]
    for a in range(3):
        pltpu.make_async_copy(sources[a].at[:, col(0)], targets[a].at[row(0), :], own_sem.at[a]).wait()
        pltpu.make_async_copy(many, many, send_sem.at[a]).wait()
        pltpu.make_async_copy(many, many, recv_sem.at[a]).wait()
    pltpu.make_async_copy(
        g_send.at[0, :, 0:HD], gh_ref.at[row(0), :], g_own_sem
    ).wait()
    pltpu.make_async_copy(many, many, g_send_sem).wait()
    pltpu.make_async_copy(many, many, g_recv_sem).wait()


def gather_in(queries, key_rows, values, upstream, out_weight):
    any_space = pl.BlockSpec(memory_space=pl.ANY)
    return pl.pallas_call(
        gather_in_kernel,
        out_shape=[jax.ShapeDtypeStruct((D, HD), BF16)] * 4,
        in_specs=[any_space] * 5,
        out_specs=[any_space] * 4,
        scratch_shapes=[
            pltpu.VMEM((8 * ROWS, WIDE), BF16),
            pltpu.VMEM((D, WIDE), BF16),
            pltpu.VMEM((8, 8 * ROWS, WIDE), BF16),
            pltpu.VMEM((8, 3, 256, WIDE), BF16),
            pltpu.VMEM((8, ROWS, WIDE), F32),
            pltpu.VMEM((8, ROWS, WIDE), BF16),
            pltpu.VMEM((8, ROWS, WIDE), BF16),
            pltpu.VMEM((8, ROWS, WIDE), BF16),
            pltpu.SemaphoreType.DMA((2,)),
            pltpu.SemaphoreType.DMA((3,)),
            pltpu.SemaphoreType.DMA((3,)),
            pltpu.SemaphoreType.DMA((3,)),
            pltpu.SemaphoreType.DMA((8, 3)),
            pltpu.SemaphoreType.DMA((8, 3)),
            pltpu.SemaphoreType.DMA((8,)),
            pltpu.SemaphoreType.DMA((8,)),
            pltpu.SemaphoreType.DMA,
            pltpu.SemaphoreType.DMA,
            pltpu.SemaphoreType.DMA,
        ],
        compiler_params=pltpu.CompilerParams(
            collective_id=0, has_side_effects=True, vmem_limit_bytes=60 << 20
        ),
        name="gather_in",
    )(queries, key_rows, values, upstream, out_weight)


def attention_kernel(
    blocks_ref, q_ref, k_ref, v_ref, g_ref, o_ref, dq_ref, dk_ref, dv_ref, dk_sum, dv_sum
):
    factor = 1.0 / math.sqrt(HD)
    dk_sum[...] = jnp.zeros_like(dk_sum)
    dv_sum[...] = jnp.zeros_like(dv_sum)

    def one(a):
        listed = [blocks_ref[a, n] for n in range(NB)]
        q = q_ref[a]
        g = g_ref[a]
        k = jnp.concatenate([k_ref[b] for b in listed], axis=0)
        v = jnp.concatenate([v_ref[b] for b in listed], axis=0)
        over_last = (((1,), (1,)), ((), ()))
        over_first = (((0,), (0,)), ((), ()))
        scores = lax.dot_general(q, k, over_last, preferred_element_type=F32) * factor
        shifted = jnp.exp(scores - jnp.max(scores, axis=-1, keepdims=True))
        soft = shifted * (1.0 / jnp.sum(shifted, axis=-1, keepdims=True))
        low = soft.astype(BF16)
        context = jnp.dot(low, v, preferred_element_type=F32).astype(BF16)
        o_ref[a] = context
        delta = jnp.sum(g.astype(F32) * context.astype(F32), axis=-1, keepdims=True)
        dprobs = lax.dot_general(g, v, over_last, preferred_element_type=F32)
        dscores = (soft * (dprobs - delta) * factor).astype(BF16)
        dq_ref[a] = jnp.dot(dscores, k, preferred_element_type=F32).astype(BF16)
        dk = lax.dot_general(dscores, q, over_first, preferred_element_type=F32)
        dv = lax.dot_general(low, g, over_first, preferred_element_type=F32)
        return listed, dk, dv

    def step(i, carry):
        done = [one(i * 4 + n) for n in range(4)]
        for listed, dk, dv in done:
            for n in range(NB):
                dk_sum[listed[n]] += dk[n * BLK : (n + 1) * BLK]
                dv_sum[listed[n]] += dv[n * BLK : (n + 1) * BLK]
        return carry

    lax.fori_loop(0, 16, step, 0)
    dk_ref[...] = dk_sum[...].astype(BF16)
    dv_ref[...] = dv_sum[...].astype(BF16)


def attention(blocks, q, k, v, g):
    count = D // BLK
    tiles = jax.ShapeDtypeStruct((count, BLK, HD), BF16)
    vmem = pl.BlockSpec(memory_space=pltpu.VMEM)
    results = pl.pallas_call(
        attention_kernel,
        out_shape=[tiles] * 4,
        in_specs=[pl.BlockSpec(memory_space=pltpu.SMEM)] + [vmem] * 4,
        out_specs=[vmem] * 4,
        scratch_shapes=[pltpu.VMEM((count, BLK, HD), F32)] * 2,
        compiler_params=pltpu.CompilerParams(vmem_limit_bytes=40 << 20),
        name="attention",
    )(blocks, *[array.reshape(count, BLK, HD) for array in (q, k, v, g)])
    return [array.reshape(D, HD) for array in results]


def spread_out_kernel(
    o_ref, dq_ref, dk_ref, dv_ref, u_ref,
    att_ref, dqt_ref, dkt_ref, dvt_ref, gw_ref,
    u_buf, every, part, c_got, x_send, x_got, keep, z_send, z_got, final,
    load_sem, a_send_sem, a_recv_sem, own_sem, send_sem, recv_sem, att_sem,
    xl_send_sem, xl_recv_sem, y_send_sem, y_recv_sem, r_send_sem, r_recv_sem,
    c_send_sem, c_recv_sem, xh_send_sem, xh_recv_sem, z_send_sem, z_recv_sem,
):
    me = lax.axis_index("seq")
    tp = lax.axis_index("tp")
    x_hi, z, core = me // 16, lax.rem(me // 2, NZ), lax.rem(me, 2)
    y, x_lo = tp // 2, lax.rem(tp, 2)
    load_u = pltpu.make_async_copy(u_ref, u_buf, load_sem)
    load_u.start()
    enter(me, tp)

    mine = every.at[z, row(tp), col(core * 2 + x_hi)]
    pltpu.make_async_copy(o_ref.at[row(me), :], mine, a_recv_sem.at[z]).start()

    def send_attended(step, carry):
        peer = seq_peer(step, me)
        pltpu.make_async_remote_copy(
            src_ref=o_ref.at[row(peer), :],
            dst_ref=mine,
            send_sem=a_send_sem,
            recv_sem=a_recv_sem.at[z],
            device_id=(peer, tp),
            device_id_type=MESH,
        ).start()
        return carry

    lax.fori_loop(1, NSEQ, send_attended, 0)
    sources = (dq_ref, dk_ref, dv_ref)
    targets = (dqt_ref, dkt_ref, dvt_ref)
    for a in range(3):
        pltpu.make_async_copy(
            sources[a].at[row(me), :], targets[a].at[:, col(me)], own_sem.at[a]
        ).start()

        def send_tokens(step, carry, a=a):
            peer = seq_peer(step, me)
            pltpu.make_async_remote_copy(
                src_ref=sources[a].at[row(peer), :],
                dst_ref=targets[a].at[:, col(me)],
                send_sem=send_sem.at[a],
                recv_sem=recv_sem.at[a],
                device_id=(peer, tp),
                device_id_type=MESH,
            ).start()
            return carry

        lax.fori_loop(1, NSEQ, send_tokens, 0)
    load_u.wait()

    def tp_copy(chunk, sequence, target, send, recv):
        here = every.at[chunk, row(sequence), :]
        return pltpu.make_async_remote_copy(
            src_ref=here,
            dst_ref=here,
            send_sem=send,
            recv_sem=recv,
            device_id=(me, target),
            device_id_type=MESH,
        )

    def xl_copy(chunk):
        return tp_copy(chunk, tp, y * 2 + 1 - x_lo, xl_send_sem.at[chunk], xl_recv_sem.at[chunk])

    def y_copy(chunk, direction, slot):
        target = lax.rem(y + (1 if direction == 0 else NY - 1), NY)
        x = x_lo if slot == 0 else 1 - x_lo
        return tp_copy(
            chunk, y * 2 + x, target * 2 + x_lo,
            y_send_sem.at[direction, slot, chunk], y_recv_sem.at[direction, slot, chunk],
        )

    def relay_copy(chunk, direction):
        target = lax.rem(y + (1 if direction == 0 else NY - 1), NY)
        origin = lax.rem(y + (NY - 1 if direction == 0 else 1), NY)
        x = x_lo if direction == 0 else 1 - x_lo
        return tp_copy(
            chunk, origin * 2 + x, target * 2 + x_lo,
            r_send_sem.at[direction, chunk], r_recv_sem.at[direction, chunk],
        )

    def att_copy(chunk, place):
        head = seq_of(place % 2, chunk, place // 2)
        return pltpu.make_async_copy(
            every.at[chunk, row(tp), place * HD : (place + 1) * HD],
            att_ref.at[:, col(head)],
            att_sem,
        )

    def c_copy(chunk):
        return pltpu.make_async_remote_copy(
            src_ref=part.at[chunk, row(1 - core, 256), :],
            dst_ref=c_got.at[chunk],
            send_sem=c_send_sem.at[chunk],
            recv_sem=c_recv_sem.at[chunk],
            device_id=(seq_of(x_hi, z, 1 - core), tp),
            device_id_type=MESH,
        )

    def xh_copy(chunk):
        return pltpu.make_async_remote_copy(
            src_ref=x_send.at[chunk],
            dst_ref=x_got.at[chunk],
            send_sem=xh_send_sem.at[chunk],
            recv_sem=xh_recv_sem.at[chunk],
            device_id=(seq_of(1 - x_hi, z, core), tp),
            device_id_type=MESH,
        )

    def z_copy(chunk):
        return pltpu.make_async_remote_copy(
            src_ref=z_send.at[chunk],
            dst_ref=z_got.at[z],
            send_sem=z_send_sem.at[chunk],
            recv_sem=z_recv_sem,
            device_id=(seq_of(x_hi, chunk, core), tp),
            device_id_type=MESH,
        )

    def stage_attended(chunk):
        here = every.at[chunk, row(tp), :]
        pltpu.make_async_copy(here, here, a_recv_sem.at[chunk]).wait()
        xl_copy(chunk).start()
        y_copy(chunk, 0, 0).start()
        y_copy(chunk, 1, 0).start()
        for place in range(4):
            att_copy(chunk, place).start()

    def stage_neighbour(chunk):
        xl_copy(chunk).wait_recv()
        y_copy(chunk, 0, 1).start()
        y_copy(chunk, 1, 1).start()

    def stage_relay(chunk):
        y_copy(chunk, 0, 0).wait_recv()
        relay_copy(chunk, 0).start()
        y_copy(chunk, 1, 1).wait_recv()
        relay_copy(chunk, 1).start()

    def stage_product(chunk):
        y_copy(chunk, 0, 1).wait_recv()
        y_copy(chunk, 1, 0).wait_recv()
        relay_copy(chunk, 0).wait_recv()
        relay_copy(chunk, 1).wait_recv()
        part[chunk] = lax.dot_general(
            every[chunk], u_buf[...], (((0,), (0,)), ((), ())), preferred_element_type=F32
        ).astype(BF16)
        c_copy(chunk).start()

    def stage_core(chunk):
        c_copy(chunk).wait_recv()

        def total(x):
            here = pl.ds(pl.multiple_of(core * 256 + x * 128, 128), 128)
            there = pl.ds(pl.multiple_of(x * 128, 128), 128)
            return part[chunk, here, :].astype(F32) + c_got[chunk, there, :].astype(F32)

        x_send[chunk] = total(1 - x_hi).astype(BF16)
        xh_copy(chunk).start()
        keep[chunk] = total(x_hi)

    def stage_x(chunk):
        xh_copy(chunk).wait_recv()
        total = keep[chunk] + x_got[chunk].astype(F32)

        @pl.when(chunk == z)
        def _():
            final[...] = total

        @pl.when(chunk != z)
        def _():
            z_send[chunk] = total.astype(BF16)
            z_copy(chunk).start()

    stages = (
        stage_attended, stage_neighbour, stage_relay, stage_product, stage_core, stage_x,
    )

    def step(j, carry):
        for lag, stage in enumerate(stages):

            @pl.when((j >= lag) & (j < lag + NZ))
            def _():
                stage(chunk_at(j - lag, z))

        return carry

    lax.fori_loop(0, NZ + len(stages) - 1, step, 0)

    def drain(chunk, carry):
        xl_copy(chunk).wait_send()
        for direction in range(2):
            for slot in range(2):
                y_copy(chunk, direction, slot).wait_send()
            relay_copy(chunk, direction).wait_send()
        c_copy(chunk).wait_send()
        xh_copy(chunk).wait_send()

        @pl.when(chunk != z)
        def _():
            z_copy(chunk).wait_send()

        return carry

    lax.fori_loop(0, NZ, drain, 0)
    seven = z_got.at[pl.ds(0, NZ - 1)]
    pltpu.make_async_copy(seven, seven, z_recv_sem).wait()

    def add(d, carry):
        final[...] += z_got[lax.rem(z + d, NZ)].astype(F32)
        return carry

    lax.fori_loop(1, NZ, add, 0)
    gw_ref[...] = final[...]
    whole = every.at[0, row(0), :]
    for chunk in range(NZ):
        pltpu.make_async_copy(whole, whole, att_sem).wait()
    many = o_ref.at[pl.ds(0, 31 * ROWS)]
    pltpu.make_async_copy(many, many, a_send_sem).wait()
    for a in range(3):
        pltpu.make_async_copy(sources[a].at[row(0), :], targets[a].at[:, col(0)], own_sem.at[a]).wait()
        pltpu.make_async_copy(many, many, send_sem.at[a]).wait()
        pltpu.make_async_copy(many, many, recv_sem.at[a]).wait()


def spread_out(attended, dq, dk, dv, upstream):
    any_space = pl.BlockSpec(memory_space=pl.ANY)
    dma = pltpu.SemaphoreType.DMA
    tokens = jax.ShapeDtypeStruct((ROWS, D), BF16)
    return pl.pallas_call(
        spread_out_kernel,
        out_shape=[tokens] * 4 + [jax.ShapeDtypeStruct((ROWS, WIDE), F32)],
        in_specs=[any_space] * 5,
        out_specs=[any_space] * 4 + [pl.BlockSpec(memory_space=pltpu.VMEM)],
        scratch_shapes=[
            pltpu.VMEM((8 * ROWS, WIDE), BF16),
            pltpu.VMEM((NZ, 8 * ROWS, WIDE), BF16),
            pltpu.VMEM((NZ, 4 * ROWS, WIDE), BF16),
            pltpu.VMEM((NZ, 2 * ROWS, WIDE), BF16),
            pltpu.VMEM((NZ, ROWS, WIDE), BF16),
            pltpu.VMEM((NZ, ROWS, WIDE), BF16),
            pltpu.VMEM((NZ, ROWS, WIDE), F32),
            pltpu.VMEM((NZ, ROWS, WIDE), BF16),
            pltpu.VMEM((NZ, ROWS, WIDE), BF16),
            pltpu.VMEM((ROWS, WIDE), F32),
            dma, dma, dma((NZ,)), dma((3,)), dma((3,)), dma((3,)), dma,
            dma((NZ,)), dma((NZ,)), dma((2, 2, NZ)), dma((2, 2, NZ)), dma((2, NZ)), dma((2, NZ)),
            dma((NZ,)), dma((NZ,)), dma((NZ,)), dma((NZ,)), dma((NZ,)), dma,
        ],
        compiler_params=pltpu.CompilerParams(
            collective_id=1, has_side_effects=True, vmem_limit_bytes=60 << 20
        ),
        name="spread_out",
    )(attended, dq, dk, dv, upstream)


def on_device(queries, key_rows, values, upstream, out_weight, blocks):
    upstream_rows = upstream.reshape(8 * ROWS, WIDE)
    heads = gather_in(queries[0], key_rows[0], values[0], upstream_rows, out_weight)
    results = attention(blocks, *heads)
    attended, dq, dk, dv, grad_weight = spread_out(*results, upstream_rows)
    return (attended[None], dq[None], dk[None], dv[None], grad_weight)


def solution(mesh):
    in_specs = (
        P("tp", "seq", None),
        P("tp", "seq", None),
        P("tp", "seq", None),
        P(None, "seq", "tp"),
        P(None, "tp"),
        P(),
    )
    out_specs = (
        P("tp", "seq", None),
        P("tp", "seq", None),
        P("tp", "seq", None),
        P("tp", "seq", None),
        P("seq", "tp"),
    )
    return jax.shard_map(
        on_device, mesh=mesh, in_specs=in_specs, out_specs=out_specs, check_vma=False
    )
```

time: 881 us -> 302 us (0.34)
  Pallas kernels: 0 us -> 280 us
  waiting for transfers between devices: 260 us -> 0 us
  other arithmetic: 243 us -> 0 us
  local copies, waits for them, and re-layouts: 174 us -> 16.9 us
  starting transfers between devices: 72.4 us -> 0 us
  matrix products: 66.6 us -> 0 us
  blocking collectives: 40.3 us -> 0 us
  between operations: 14.3 us -> 0.71 us
    pallas_call x0 -> x3, Pallas kernels: none -> 280 us  [the longest x1 120 us: spread_out(): pl.pallas_call(spread_out_kernel, out_shape=[tokens] * 4 + [jax.ShapeDtyp...]
    unnamed x8 -> x0, other arithmetic: 185 us -> none
    all_gather x1 -> x0, waiting for transfers between devices: 159 us -> none  [on_device(): every_sequence = lax.all_gather(attended, 'tp', axis=0, tiled=True)]
    reduce_scatter x2 -> x0, waiting for transfers between devices: 84 us -> none  [the longest x1 84 us: on_device(): lax.psum_scatter(jnp.einsum('stc,dc->std', upstream, out_weight, preferre...]
    all_to_all x7 -> x0, starting transfers between devices: 72.2 us -> none  [the longest x1 11.6 us: on_device(): lax.all_to_all(values, 'seq', split_axis=2, concat_axis=1, tiled=True)]
    another operation x6 -> x0, local copies, waits for them, and re-layouts: 68.2 us -> none  [the longest x4 67.7 us: join_heads(): return array.reshape(count_heads, length, HD).transpose(1, 0, 2).reshape(...]
    unnamed x43 -> x28, local copies, waits for them, and re-layouts: 84.4 us -> 16.9 us
    dot_general x8 -> x0, matrix products: 66.6 us -> none  [the longest x1 14.2 us: backward_head(): jnp.einsum('qij,qid->qjd', probs_low, grad_tiles, preferred_element_type=...]
  transfers between devices with their start and end apart: 10 -> 0, of which waited for: 4 -> 0; matrix products, arithmetic and copies ran while one was open for 45% -> 0% of each run, Pallas kernels for 0% -> 0%
where the time goes in v1:
time: 302 us; the launch traced here: 298 us
  Pallas kernels  280 us (93%)
  local copies, waits for them, and re-layouts  16.9 us (6%)
    pallas_call x1, Pallas kernels, spread_out(): pl.pallas_call(spread_out_kernel, out_shape=[tokens] * 4 + [jax.ShapeDtyp...  120 us
    pallas_call x1, Pallas kernels, gather_in(): pl.pallas_call(gather_in_kernel, out_shape=[jax.ShapeDtypeStruct((D, HD),...  117 us
    pallas_call x1, Pallas kernels, attention(): pl.pallas_call(attention_kernel, out_shape=[tiles] * 4, in_specs=[pl.Bloc...  43.5 us
    unnamed x28, local copies, waits for them, and re-layouts  16.9 us

profile of v1, /device:TPU:32, one launch (start us, length us, event | category | flops | bytes accessed | tf_op | source)
XLA Modules:
  0.0 297.8 jit_solution(17432209829201294873)
XLA Ops:
  0.6 0.8 copy.11.blocks_ref
  1.4 116.8 %gather_in.1 = (bf16[4096,128]{1,0:T(8,128)(2,1)}, bf16[4096,128]{1,0:T(8,128)(2,1)}, bf16[4096,128]{1,0:T(8,128)(2,1)}, bf16[4096,128]{1,0:T(8,128)(2,1)}) custom-call(bf16[128,4096]{1,0:T(8,128)(2,1)} %bitcast.30, bf16[128,4096]{1,0:T(8,128)(2,1)} %bitcast.31, bf16[128,4096]{1,0:T(8,128)(2,1)} %bitcast.32, bf16[1024,512]{1,0:T(8,128)(2,1)} %bitcast.24, ...), custom_call_target="tpu_custom_call" | custom-call | tf_op jit(solution)/shard_map/gather_in/pallas_call | solution.py:224
  118.2 0.0 copy-start.4
  118.2 1.2 copy-done.4
  119.4 0.0 copy-start.5
  119.4 1.2 copy-done.5
  120.6 0.0 copy-start.6
  120.6 1.2 copy-done.6
  121.8 0.0 copy-start.7
  121.8 1.2 copy-done.7
  123.1 43.5 %attention.1 = (bf16[64,64,128]{2,1,0:T(8,128)(2,1)S(1)}, bf16[64,64,128]{2,1,0:T(8,128)(2,1)S(1)}, bf16[64,64,128]{2,1,0:T(8,128)(2,1)S(1)}, bf16[64,64,128]{2,1,0:T(8,128)(2,1)S(1)}) custom-call(s32[64,4]{1,0:T(8,128)S(1)} %copy.11.blocks_ref, bf16[64,64,128]{2,1,0:T(8,128)(2,1)S(1)} %bitcast.20, bf16[64,64,128]{2,1,0:T(8,128)(2,1)S(1)} %bitcast.21, ...), custom_call_target="tpu_custom_call" | custom-call | tf_op jit(solution)/shard_map/attention/pallas_call | solution.py:303
  166.6 0.0 copy-start
  166.6 1.0 copy-done
  167.5 0.0 copy-start.1
  167.5 1.0 copy-done.1
  168.5 0.0 copy-start.2
  168.5 1.0 copy-done.2
  169.5 0.0 copy-start.3
  169.5 1.0 copy-done.3
  170.4 120.0 %spread_out.1 = (bf16[128,4096]{1,0:T(8,128)(2,1)}, bf16[128,4096]{1,0:T(8,128)(2,1)}, bf16[128,4096]{1,0:T(8,128)(2,1)}, bf16[128,4096]{1,0:T(8,128)(2,1)}, f32[128,512]{1,0:T(8,128)}) custom-call(bf16[4096,128]{1,0:T(8,128)(2,1)} %bitcast.16, bf16[4096,128]{1,0:T(8,128)(2,1)} %bitcast.17, bf16[4096,128]{1,0:T(8,128)(2,1)} %bitcast.18, ...), custom_call_target="tpu_custom_call" | custom-call | tf_op jit(solution)/shard_map/spread_out/pallas_call | solution.py:548
  290.4 0.0 copy-start.9
  290.5 0.0 copy-start.8
  290.5 0.0 copy-start.10
  290.5 2.4 copy.17
  292.9 2.3 copy.18
  295.2 0.0 copy-done.9
  295.2 1.0 copy.19
  296.2 0.0 copy-done.8
  296.2 1.0 copy.20
  297.1 0.0 copy-done.10
  297.1 0.7 copy.21
Async XLA Ops:
  118.2 1.2 copy-start.4
  119.4 1.2 copy-start.5
  120.6 1.2 copy-start.6
  121.8 1.2 copy-start.7
  166.6 1.0 copy-start
  167.5 1.0 copy-start.1
  168.5 1.0 copy-start.2
  169.5 1.0 copy-start.3
  290.4 4.8 %copy-start.9 = (bf16[128,4096]{1,0:T(8,128)(2,1)S(1)}, bf16[128,4096]{1,0:T(8,128)(2,1)}, u32[]{:S(2)}) copy-start(bf16[128,4096]{1,0:T(8,128)(2,1)} %get-tuple-element.28) | copy-start | bytes 3145732
  290.5 5.7 %copy-start.8 = (bf16[128,4096]{1,0:T(8,128)(2,1)S(1)}, bf16[128,4096]{1,0:T(8,128)(2,1)}, u32[]{:S(2)}) copy-start(bf16[128,4096]{1,0:T(8,128)(2,1)} %get-tuple-element.29) | copy-start | bytes 3145732
  290.5 6.7 %copy-start.10 = (f32[128,512]{1,0:T(8,128)S(1)}, f32[128,512]{1,0:T(8,128)}, u32[]{:S(2)}) copy-start(f32[128,512]{1,0:T(8,128)} %get-tuple-element.40) | copy-start | bytes 786436

commit v2 on v1

v2 whole, which is shorter than its diff:
```python
import functools
import math

import jax
import jax.numpy as jnp
from jax import lax
from jax.experimental import pallas as pl
from jax.experimental.pallas import tpu as pltpu
from jax.sharding import PartitionSpec as P

HD = 128
BLK = 64
NB = 4
MESH = pl.DeviceIdType.MESH
BF16 = jnp.bfloat16
F32 = jnp.float32

NZ = 8
NY = 4
NSEQ = 32
ROWS = 128
WIDE = 512
D = 4096


def seq_of(x_hi, z, core):
    return x_hi * 16 + z * 2 + core


def near_far(step, place, count):
    half = (step + 1) // 2
    return lax.rem(jnp.where(lax.rem(step, 2) == 1, place + half, place + count - half), count)


def seq_peer(step, me):
    z = near_far(step // 4, lax.rem(me // 2, NZ), NZ)
    x_hi = lax.rem(me // 16 + lax.rem(step, 2), 2)
    core = lax.rem(lax.rem(me, 2) + lax.rem(step // 2, 2), 2)
    return seq_of(x_hi, z, core)


def col(index):
    return pl.ds(pl.multiple_of(index * HD, HD), HD)


def row(index, size=ROWS):
    return pl.ds(pl.multiple_of(index * size, size), size)


def chunk_at(step, z):
    return near_far(NZ - 1 - step, z, NZ)


def enter(me, tp):
    barrier = pltpu.get_barrier_semaphore()

    def greet_seq(d, carry):
        pl.semaphore_signal(
            barrier, inc=1, device_id=(lax.rem(me + d, NSEQ), tp), device_id_type=MESH
        )
        return carry

    def greet_tp(d, carry):
        pl.semaphore_signal(
            barrier, inc=1, device_id=(me, lax.rem(tp + d, 8)), device_id_type=MESH
        )
        return carry

    lax.fori_loop(1, NSEQ, greet_seq, 0)
    lax.fori_loop(1, 8, greet_tp, 0)
    pl.semaphore_wait(barrier, NSEQ - 1 + 7)


OVER_LAST = (((1,), (1,)), ((), ()))
OVER_FIRST = (((0,), (0,)), ((), ()))
FACTOR = 1.0 / math.sqrt(HD)


def whole_kernel(
    table_ref, q_ref, k_ref, v_ref, u_ref, w_ref,
    att_ref, dqt_ref, dkt_ref, dvt_ref, gw_ref,
    u_buf, w_buf, terms, y_got, keep, x_send, x_got, g_send,
    qh, kh, vh, gh, o_buf, dq_buf, dk_buf, dv_buf, soft_buf, dk_sum, dv_sum, dk_far, dv_far,
    every, c_got, xh_got, z_got, final,
    load_sem, own_sem, send_sem, recv_sem, ty_send_sem, ty_recv_sem, tx_send_sem, tx_recv_sem,
    g_send_sem, g_recv_sem,
    a_send_sem, a_recv_sem, d_own_sem, d_send_sem, d_recv_sem, att_sem,
    xl_send_sem, xl_recv_sem, y_send_sem, y_recv_sem, r_send_sem, r_recv_sem,
    c_send_sem, c_recv_sem, xh_send_sem, xh_recv_sem, z_send_sem, z_recv_sem,
):
    me = lax.axis_index("seq")
    tp = lax.axis_index("tp")
    x_hi, z, core = me // 16, lax.rem(me // 2, NZ), lax.rem(me, 2)
    y, x_lo = tp // 2, lax.rem(tp, 2)
    load_u = pltpu.make_async_copy(u_ref, u_buf, load_sem.at[0])
    load_w = pltpu.make_async_copy(w_ref, w_buf, load_sem.at[1])
    load_u.start()
    load_w.start()
    enter(me, tp)

    def send_heads(a):
        source, target = (q_ref, k_ref, v_ref)[a], (qh, kh, vh)[a]
        place = target.at[pl.ds(2 * me, 2)]
        pltpu.make_async_copy(source.at[:, :, col(me)], place, own_sem.at[a]).start()

        def send(step, carry):
            peer = seq_peer(step, me)
            pltpu.make_async_remote_copy(
                src_ref=source.at[:, :, col(peer)],
                dst_ref=place,
                send_sem=send_sem.at[a],
                recv_sem=recv_sem.at[a],
                device_id=(peer, tp),
                device_id_type=MESH,
            ).start()
            return carry

        lax.fori_loop(1, NSEQ, send, 0)

    def ty_copy(j, d):
        other = lax.rem(y + d, NY)
        return pltpu.make_async_remote_copy(
            src_ref=terms.at[j, row(other, 256), :],
            dst_ref=y_got.at[j, d - 1],
            send_sem=ty_send_sem.at[j, d - 1],
            recv_sem=ty_recv_sem.at[j, d - 1],
            device_id=(me, other * 2 + x_lo),
            device_id_type=MESH,
        )

    def tx_copy(j):
        return pltpu.make_async_remote_copy(
            src_ref=x_send.at[j],
            dst_ref=x_got.at[j],
            send_sem=tx_send_sem.at[j],
            recv_sem=tx_recv_sem.at[j],
            device_id=(me, y * 2 + 1 - x_lo),
            device_id_type=MESH,
        )

    def stage_terms(j):
        chunk = chunk_at(j, z)
        for half in range(2):
            rows = pl.ds(pl.multiple_of(half * 2048 + chunk * 256, 256), 256)
            terms[j, :, half * 256 : (half + 1) * 256] = lax.dot_general(
                u_buf[...], w_buf[rows, :], OVER_LAST, preferred_element_type=F32
            ).astype(BF16)
        for d in (2, 1, 3):
            ty_copy(j, d).start()

    def stage_ty(j):
        for d in (1, 2, 3):
            ty_copy(j, d).wait_recv()

        def total(x):
            rows = pl.ds(pl.multiple_of(y * 256 + x * 128, 128), 128)
            here = pl.ds(pl.multiple_of(x * 128, 128), 128)
            result = terms[j, rows, :].astype(F32)
            for d in range(3):
                result = result + y_got[j, d, here, :].astype(F32)
            return result

        x_send[j] = total(1 - x_lo).astype(BF16)
        tx_copy(j).start()
        keep[j] = total(x_lo)

    def stage_tx(j):
        tx_copy(j).wait_recv()
        g_send[j] = (keep[j] + x_got[j].astype(F32)).astype(BF16)
        chunk = chunk_at(j, z)
        for place in range(4):
            peer = seq_of(place // 2, chunk, place % 2)
            source = g_send.at[j, :, place * HD : (place + 1) * HD]
            target = gh.at[row(me), :]

            @pl.when(peer == me)
            def _():
                pltpu.make_async_copy(source, target, own_sem.at[3]).start()

            @pl.when(peer != me)
            def _():
                pltpu.make_async_remote_copy(
                    src_ref=source,
                    dst_ref=target,
                    send_sem=g_send_sem,
                    recv_sem=g_recv_sem,
                    device_id=(peer, tp),
                    device_id_type=MESH,
                ).start()

    def block_at(n):
        return 2 * seq_peer(n // 2, me) + lax.rem(n, 2)

    def tile(a):
        return pl.ds(pl.multiple_of(a * BLK, BLK), BLK)

    def window(a):
        return (lax.rem(a + 63, 64), a, lax.rem(a + 1, 64))

    def key_set(ref, a):
        return jnp.concatenate([ref[b] for b in window(a) + (table_ref[a],)], axis=0)

    def send_rows(source, target, sem_send, sem_recv, sem_own, i):
        peer = seq_peer(i, me)

        @pl.when(i == 0)
        def _():
            pltpu.make_async_copy(source.at[row(me), :], target, sem_own).start()

        @pl.when(i > 0)
        def _():
            pltpu.make_async_remote_copy(
                src_ref=source.at[row(peer), :],
                dst_ref=target,
                send_sem=sem_send,
                recv_sem=sem_recv,
                device_id=(peer, tp),
                device_id_type=MESH,
            ).start()

    my_place = every.at[z, row(tp), col(core * 2 + x_hi)]

    def forward_one(a):
        k, v = key_set(kh, a), key_set(vh, a)
        scores = lax.dot_general(qh[a], k, OVER_LAST, preferred_element_type=F32) * FACTOR
        shifted = jnp.exp(scores - jnp.max(scores, axis=-1, keepdims=True))
        soft = shifted * (1.0 / jnp.sum(shifted, axis=-1, keepdims=True))
        soft_buf[tile(a), :] = soft
        o_buf[tile(a), :] = jnp.dot(soft.astype(BF16), v, preferred_element_type=F32).astype(BF16)

    def forward_pair(i, carry):
        for m in range(4):
            forward_one(block_at(i * 4 + m))
        for m in range(2):
            send_rows(o_buf, my_place, a_send_sem, a_recv_sem.at[z], a_recv_sem.at[z], i * 2 + m)
        return carry

    def backward_one(a):
        q, g = qh[a], gh[tile(a), :]
        k, v = key_set(kh, a), key_set(vh, a)
        soft = soft_buf[tile(a), :]
        context = o_buf[tile(a), :]
        delta = jnp.sum(g.astype(F32) * context.astype(F32), axis=-1, keepdims=True)
        dprobs = lax.dot_general(g, v, OVER_LAST, preferred_element_type=F32)
        dscores = (soft * (dprobs - delta) * FACTOR).astype(BF16)
        dq_buf[tile(a), :] = jnp.dot(dscores, k, preferred_element_type=F32).astype(BF16)
        dk = lax.dot_general(dscores, q, OVER_FIRST, preferred_element_type=F32)
        dv = lax.dot_general(soft.astype(BF16), g, OVER_FIRST, preferred_element_type=F32)
        return dk, dv

    def backward_pair(i):
        places = [i * 4 + m for m in range(4)]
        done = [backward_one(block_at(n)) for n in places]
        for n, (dk, dv) in zip(places, done):
            near = window(block_at(n))
            for m in range(3):
                dk_sum[tile(near[m]), :] += dk[m * BLK : (m + 1) * BLK]
                dv_sum[tile(near[m]), :] += dv[m * BLK : (m + 1) * BLK]
            dk_far[block_at(n) + 1] = dk[3 * BLK :]
            dv_far[block_at(n) + 1] = dv[3 * BLK :]
        for m in range(2):
            send_rows(
                dq_buf, dqt_ref.at[:, col(me)],
                d_send_sem.at[0], d_recv_sem.at[0], d_own_sem.at[0], i * 2 + m,
            )

    def link_far(a, carry):
        before = table_ref[64 + a]
        dk_far[a + 1] += dk_far[before]
        dv_far[a + 1] += dv_far[before]
        return carry

    def finish_keys(i, carry):
        for m in range(2):
            b = 2 * seq_peer(i, me) + m
            dk_buf[tile(b), :] = (dk_sum[tile(b), :] + dk_far[table_ref[128 + b]]).astype(BF16)
            dv_buf[tile(b), :] = (dv_sum[tile(b), :] + dv_far[table_ref[128 + b]]).astype(BF16)
        for n, (source, target) in enumerate(((dk_buf, dkt_ref), (dv_buf, dvt_ref))):
            send_rows(
                source, target.at[:, col(me)],
                d_send_sem.at[n + 1], d_recv_sem.at[n + 1], d_own_sem.at[n + 1], i,
            )
        return carry

    def tp_copy(chunk, sequence, target, send, recv):
        here = every.at[chunk, row(sequence), :]
        return pltpu.make_async_remote_copy(
            src_ref=here,
            dst_ref=here,
            send_sem=send,
            recv_sem=recv,
            device_id=(me, target),
            device_id_type=MESH,
        )

    def xl_copy(chunk):
        return tp_copy(chunk, tp, y * 2 + 1 - x_lo, xl_send_sem.at[chunk], xl_recv_sem.at[chunk])

    def y_copy(chunk, direction, slot):
        target = lax.rem(y + (1 if direction == 0 else NY - 1), NY)
        x = x_lo if slot == 0 else 1 - x_lo
        return tp_copy(
            chunk, y * 2 + x, target * 2 + x_lo,
            y_send_sem.at[direction, slot, chunk], y_recv_sem.at[direction, slot, chunk],
        )

    def relay_copy(chunk, direction):
        target = lax.rem(y + (1 if direction == 0 else NY - 1), NY)
        origin = lax.rem(y + (NY - 1 if direction == 0 else 1), NY)
        x = x_lo if direction == 0 else 1 - x_lo
        return tp_copy(
            chunk, origin * 2 + x, target * 2 + x_lo,
            r_send_sem.at[direction, chunk], r_recv_sem.at[direction, chunk],
        )

    def att_copy(chunk, place):
        head = seq_of(place % 2, chunk, place // 2)
        return pltpu.make_async_copy(
            every.at[chunk, row(tp), place * HD : (place + 1) * HD],
            att_ref.at[:, col(head)],
            att_sem,
        )

    def c_copy(chunk):
        return pltpu.make_async_remote_copy(
            src_ref=terms.at[chunk, row(1 - core, 256), :],
            dst_ref=c_got.at[chunk],
            send_sem=c_send_sem.at[chunk],
            recv_sem=c_recv_sem.at[chunk],
            device_id=(seq_of(x_hi, z, 1 - core), tp),
            device_id_type=MESH,
        )

    def xh_copy(chunk):
        return pltpu.make_async_remote_copy(
            src_ref=x_send.at[chunk],
            dst_ref=xh_got.at[chunk],
            send_sem=xh_send_sem.at[chunk],
            recv_sem=xh_recv_sem.at[chunk],
            device_id=(seq_of(1 - x_hi, z, core), tp),
            device_id_type=MESH,
        )

    def z_copy(chunk):
        return pltpu.make_async_remote_copy(
            src_ref=g_send.at[chunk],
            dst_ref=z_got.at[z],
            send_sem=z_send_sem.at[chunk],
            recv_sem=z_recv_sem,
            device_id=(seq_of(x_hi, chunk, core), tp),
            device_id_type=MESH,
        )

    def stage_attended(chunk):
        here = every.at[chunk, row(tp), :]
        pltpu.make_async_copy(here, here, a_recv_sem.at[chunk]).wait()
        xl_copy(chunk).start()
        y_copy(chunk, 0, 0).start()
        y_copy(chunk, 1, 0).start()
        for place in range(4):
            att_copy(chunk, place).start()

    def stage_neighbour(chunk):
        xl_copy(chunk).wait_recv()
        y_copy(chunk, 0, 1).start()
        y_copy(chunk, 1, 1).start()

    def stage_relay(chunk):
        y_copy(chunk, 0, 0).wait_recv()
        relay_copy(chunk, 0).start()
        y_copy(chunk, 1, 1).wait_recv()
        relay_copy(chunk, 1).start()

    def stage_product(chunk):
        y_copy(chunk, 0, 1).wait_recv()
        y_copy(chunk, 1, 0).wait_recv()
        relay_copy(chunk, 0).wait_recv()
        relay_copy(chunk, 1).wait_recv()
        terms[chunk, 0:WIDE, :] = lax.dot_general(
            every[chunk], u_buf[...], OVER_FIRST, preferred_element_type=F32
        ).astype(BF16)
        c_copy(chunk).start()

    def stage_core(chunk):
        c_copy(chunk).wait_recv()

        def total(x):
            here = pl.ds(pl.multiple_of(core * 256 + x * 128, 128), 128)
            there = pl.ds(pl.multiple_of(x * 128, 128), 128)
            return terms[chunk, here, :].astype(F32) + c_got[chunk, there, :].astype(F32)

        x_send[chunk] = total(1 - x_hi).astype(BF16)
        xh_copy(chunk).start()
        keep[chunk] = total(x_hi)

    def stage_xh(chunk):
        xh_copy(chunk).wait_recv()
        total = keep[chunk] + xh_got[chunk].astype(F32)

        @pl.when(chunk == z)
        def _():
            final[...] = total

        @pl.when(chunk != z)
        def _():
            g_send[chunk] = total.astype(BF16)
            z_copy(chunk).start()

    def when_in(s, low, high, stage):
        @pl.when((s >= low) & (s < high))
        def _():
            stage(near_far(s, z, NZ))

    send_heads(0)
    load_u.wait()
    load_w.wait()
    stage_terms(0)
    send_heads(1)
    stage_terms(1)
    send_heads(2)
    dk_sum[...] = jnp.zeros_like(dk_sum)
    dv_sum[...] = jnp.zeros_like(dv_sum)
    dk_far[...] = jnp.zeros_like(dk_far)
    dv_far[...] = jnp.zeros_like(dv_far)

    def way_in(j, carry):
        @pl.when(j < 8)
        def _():
            stage_terms(j)

        stage_ty(j - 2)

        @pl.when(j >= 3)
        def _():
            stage_tx(j - 3)

        return carry

    lax.fori_loop(2, 8, way_in, 0)
    stage_tx(5)
    many = o_buf.at[pl.ds(0, 31 * ROWS)]
    for a in range(3):
        source, target = (q_ref, k_ref, v_ref)[a], (qh, kh, vh)[a]
        pltpu.make_async_copy(source.at[:, :, col(0)], target.at[pl.ds(0, 2)], own_sem.at[a]).wait()
        pltpu.make_async_copy(many, many, recv_sem.at[a]).wait()

    def forward_part(part, carry):
        lax.fori_loop(part * 4, part * 4 + 4, forward_pair, 0)

        @pl.when(part == 0)
        def _():
            stage_ty(6)

        @pl.when(part == 1)
        def _():
            stage_tx(6)

        return carry

    lax.fori_loop(0, 4, forward_part, 0)
    stage_ty(7)
    stage_tx(7)
    pltpu.make_async_copy(g_send.at[0, :, 0:HD], gh.at[row(0), :], own_sem.at[3]).wait()
    pltpu.make_async_copy(many, many, g_recv_sem).wait()

    def backward_part(i, carry):
        backward_pair(i)

        @pl.when(lax.rem(i, 2) == 1)
        def _():
            s = i // 2
            stage_attended(near_far(s, z, NZ))
            when_in(s - 1, 0, NZ, stage_neighbour)
            when_in(s - 5, 0, NZ, stage_relay)

        return carry

    lax.fori_loop(0, 16, backward_part, 0)
    lax.fori_loop(0, D // BLK, link_far, 0)
    lax.fori_loop(0, NSEQ, finish_keys, 0)
    stage_neighbour(near_far(NZ - 1, z, NZ))

    def drain_in(j, carry):
        for d in (1, 2, 3):
            ty_copy(j, d).wait_send()
        tx_copy(j).wait_send()
        return carry

    lax.fori_loop(0, 8, drain_in, 0)
    for a in range(3):
        pltpu.make_async_copy(many, many, send_sem.at[a]).wait()
    pltpu.make_async_copy(many, many, g_send_sem).wait()

    def way_out(s, carry):
        when_in(s + 3, 3, NZ, stage_relay)
        when_in(s, 0, NZ, stage_product)
        when_in(s - 1, 0, NZ, stage_core)
        when_in(s - 2, 0, NZ, stage_xh)
        return carry

    lax.fori_loop(0, NZ + 2, way_out, 0)

    def drain_out(chunk, carry):
        xl_copy(chunk).wait_send()
        for direction in range(2):
            for slot in range(2):
                y_copy(chunk, direction, slot).wait_send()
            relay_copy(chunk, direction).wait_send()
        c_copy(chunk).wait_send()
        xh_copy(chunk).wait_send()

        @pl.when(chunk != z)
        def _():
            z_copy(chunk).wait_send()

        return carry

    lax.fori_loop(0, NZ, drain_out, 0)
    seven = z_got.at[pl.ds(0, NZ - 1)]
    pltpu.make_async_copy(seven, seven, z_recv_sem).wait()

    def add(d, carry):
        final[...] += z_got[lax.rem(z + d, NZ)].astype(F32)
        return carry

    lax.fori_loop(1, NZ, add, 0)
    gw_ref[...] = final[...]
    whole = every.at[0, row(0), :]
    for chunk in range(NZ):
        pltpu.make_async_copy(whole, whole, att_sem).wait()
    pltpu.make_async_copy(many, many, a_send_sem).wait()
    for a in range(3):
        target = (dqt_ref, dkt_ref, dvt_ref)[a]
        pltpu.make_async_copy(dq_buf.at[row(0), :], target.at[:, col(0)], d_own_sem.at[a]).wait()
        pltpu.make_async_copy(many, many, d_send_sem.at[a]).wait()
        pltpu.make_async_copy(many, many, d_recv_sem.at[a]).wait()


def whole(table, queries, key_rows, values, upstream, out_weight):
    any_space = pl.BlockSpec(memory_space=pl.ANY)
    dma = pltpu.SemaphoreType.DMA
    tokens = jax.ShapeDtypeStruct((ROWS, D), BF16)
    head = pltpu.VMEM((D, HD), BF16)
    tiles = pltpu.VMEM((D // BLK, BLK, HD), BF16)
    head_sum = pltpu.VMEM((D, HD), F32)
    far_sum = pltpu.VMEM((D // BLK + 1, BLK, HD), F32)
    piece = pltpu.VMEM((NZ, ROWS, WIDE), BF16)
    return pl.pallas_call(
        whole_kernel,
        out_shape=[tokens] * 4 + [jax.ShapeDtypeStruct((ROWS, WIDE), F32)],
        in_specs=[pl.BlockSpec(memory_space=pltpu.SMEM)] + [any_space] * 5,
        out_specs=[any_space] * 4 + [pl.BlockSpec(memory_space=pltpu.VMEM)],
        scratch_shapes=[
            pltpu.VMEM((8 * ROWS, WIDE), BF16),
            pltpu.VMEM((D, WIDE), BF16),
            pltpu.VMEM((8, 8 * ROWS, WIDE), BF16),
            pltpu.VMEM((8, 3, 256, WIDE), BF16),
            pltpu.VMEM((8, ROWS, WIDE), F32),
            piece, piece, piece,
            tiles, tiles, tiles, head, head, head, head, head,
            pltpu.VMEM((D, NB * BLK), F32),
            head_sum, head_sum, far_sum, far_sum,
            pltpu.VMEM((NZ, 8 * ROWS, WIDE), BF16),
            pltpu.VMEM((NZ, 2 * ROWS, WIDE), BF16),
            piece, piece,
            pltpu.VMEM((ROWS, WIDE), F32),
            dma((2,)), dma((4,)), dma((3,)), dma((3,)), dma((8, 3)), dma((8, 3)), dma((8,)), dma((8,)),
            dma, dma,
            dma, dma((NZ,)), dma((3,)), dma((3,)), dma((3,)), dma,
            dma((NZ,)), dma((NZ,)), dma((2, 2, NZ)), dma((2, 2, NZ)), dma((2, NZ)), dma((2, NZ)),
            dma((NZ,)), dma((NZ,)), dma((NZ,)), dma((NZ,)), dma((NZ,)), dma,
        ],
        compiler_params=pltpu.CompilerParams(
            collective_id=0, has_side_effects=True, vmem_limit_bytes=63 << 20
        ),
        name="whole",
    )(table, queries, key_rows, values, upstream, out_weight)


def far_table(blocks):
    count = blocks.shape[0]
    far = blocks[:, NB - 1][None, :]
    across = lax.broadcasted_iota(jnp.int32, (3 * count, count), 1)
    down = lax.broadcasted_iota(jnp.int32, (3 * count, count), 0)
    own = jnp.tile(blocks[:, NB - 1], 3)[:, None]
    kind, place = down // count, down % count
    value = jnp.where(
        kind == 0,
        jnp.where(across == place, far, 0),
        jnp.where(
            kind == 1,
            jnp.where((far == own) & (across < place), across + 1, 0),
            jnp.where(far == place, across + 1, 0),
        ),
    )
    return jnp.max(value, axis=1)


def on_device(queries, key_rows, values, upstream, out_weight, blocks):
    pairs = [array.reshape(2, BLK, D) for array in (queries, key_rows, values)]
    attended, dq, dk, dv, grad_weight = whole(
        far_table(blocks), *pairs, upstream.reshape(8 * ROWS, WIDE), out_weight
    )
    return (attended[None], dq[None], dk[None], dv[None], grad_weight)


def solution(mesh):
    in_specs = (
        P("tp", "seq", None),
        P("tp", "seq", None),
        P("tp", "seq", None),
        P(None, "seq", "tp"),
        P(None, "tp"),
        P(),
    )
    out_specs = (
        P("tp", "seq", None),
        P("tp", "seq", None),
        P("tp", "seq", None),
        P("tp", "seq", None),
        P("seq", "tp"),
    )
    return jax.shard_map(
        on_device, mesh=mesh, in_specs=in_specs, out_specs=out_specs, check_vma=False
    )
```

time: 302 us -> 250 us (0.83)
  Pallas kernels: 280 us -> 236 us
  local copies, waits for them, and re-layouts: 16.9 us -> 8.15 us
    pallas_call x3 -> x1, Pallas kernels: 280 us -> 236 us  [whole(): pl.pallas_call(whole_kernel, out_shape=[tokens] * 4 + [jax.ShapeDtypeStru...]
    unnamed x28 -> x11, local copies, waits for them, and re-layouts: 16.9 us -> 7.38 us
where the time goes in v2:
time: 250 us; the launch traced here: 245 us
  Pallas kernels  236 us (94%)
  local copies, waits for them, and re-layouts  8.15 us (3%)
    pallas_call x1, Pallas kernels, whole(): pl.pallas_call(whole_kernel, out_shape=[tokens] * 4 + [jax.ShapeDtypeStru...  236 us
    unnamed x11, local copies, waits for them, and re-layouts  7.38 us

profile of v2, /device:TPU:32, one launch (start us, length us, event | category | flops | bytes accessed | tf_op | source)
XLA Modules:
  0.0 245.3 jit_solution(7153855763894805627)
XLA Ops:
  0.6 0.7 slice_bitcast_fusion
  1.3 0.1 eq.34
  1.4 0.7 select_reduce_fusion.table_ref
  2.1 235.8 %whole.1 = (bf16[128,4096]{1,0:T(8,128)(2,1)}, bf16[128,4096]{1,0:T(8,128)(2,1)}, bf16[128,4096]{1,0:T(8,128)(2,1)}, bf16[128,4096]{1,0:T(8,128)(2,1)}, f32[128,512]{1,0:T(8,128)}) custom-call(s32[192]{0:T(256)} %select_reduce_fusion.table_ref, bf16[2,64,4096]{2,1,0:T(8,128)(2,1)} %bitcast.10, bf16[2,64,4096]{2,1,0:T(8,128)(2,1)} %bitcast.11, ...), custom_call_target="tpu_custom_call" | custom-call | tf_op jit(solution)/shard_map/whole/pallas_call | solution.py:548
  237.9 0.0 copy-start.1
  237.9 0.0 copy-start
  237.9 0.0 copy-start.2
  238.0 2.4 copy.16
  240.4 2.3 copy.17
  242.7 0.0 copy-done.1
  242.7 1.0 copy.18
  243.7 0.0 copy-done
  243.7 1.0 copy.19
  244.6 0.0 copy-done.2
  244.6 0.7 copy.20
  (5 shorter events, 0.0 us)
Async XLA Ops:
  237.9 4.8 %copy-start.1 = (bf16[128,4096]{1,0:T(8,128)(2,1)S(1)}, bf16[128,4096]{1,0:T(8,128)(2,1)}, u32[]{:S(2)}) copy-start(bf16[128,4096]{1,0:T(8,128)(2,1)} %get-tuple-element.12) | copy-start | bytes 3145732
  237.9 5.7 %copy-start = (bf16[128,4096]{1,0:T(8,128)(2,1)S(1)}, bf16[128,4096]{1,0:T(8,128)(2,1)}, u32[]{:S(2)}) copy-start(bf16[128,4096]{1,0:T(8,128)(2,1)} %get-tuple-element.13) | copy-start | bytes 3145732
  237.9 6.7 %copy-start.2 = (f32[128,512]{1,0:T(8,128)S(1)}, f32[128,512]{1,0:T(8,128)}, u32[]{:S(2)}) copy-start(f32[128,512]{1,0:T(8,128)} %get-tuple-element.30) | copy-start | bytes 786436

commit v3 on v2

--- a/solution.py
+++ b/solution.py
@@ -117,14 +117,21 @@
 
         lax.fori_loop(1, NSEQ, send, 0)
 
-    def ty_copy(j, d):
-        other = lax.rem(y + d, NY)
+    up, down = lax.rem(y + 1, NY), lax.rem(y + NY - 1, NY)
+    across = lax.rem(y + 2, NY)
+
+    def term_rows(target, x):
+        return pl.ds(pl.multiple_of(target * 256 + x * 128, 128), 128)
+
+    def ty_copy(j, h):
+        to = (down, up, up, down, down, up)[h]
+        goal = across if h >= 4 else to
         return pltpu.make_async_remote_copy(
-            src_ref=terms.at[j, row(other, 256), :],
-            dst_ref=y_got.at[j, d - 1],
-            send_sem=ty_send_sem.at[j, d - 1],
-            recv_sem=ty_recv_sem.at[j, d - 1],
-            device_id=(me, other * 2 + x_lo),
+            src_ref=terms.at[j, term_rows(goal, h % 2), :],
+            dst_ref=y_got.at[j, h],
+            send_sem=ty_send_sem.at[j, h],
+            recv_sem=ty_recv_sem.at[j, h],
+            device_id=(me, to * 2 + x_lo),
             device_id_type=MESH,
         )
 
@@ -145,20 +152,28 @@
             terms[j, :, half * 256 : (half + 1) * 256] = lax.dot_general(
                 u_buf[...], w_buf[rows, :], OVER_LAST, preferred_element_type=F32
             ).astype(BF16)
-        for d in (2, 1, 3):
-            ty_copy(j, d).start()
+        for h in (4, 5, 2, 3):
+            ty_copy(j, h).start()
+
+    def stage_second(j):
+        for h in (0, 1):
+            ty_copy(j, 4 + h).wait_recv()
+            rows = term_rows((down, up)[h], h)
+            terms[j, rows, :] = (
+                terms[j, rows, :].astype(F32) + y_got[j, 4 + h].astype(F32)
+            ).astype(BF16)
+            ty_copy(j, h).start()
 
     def stage_ty(j):
-        for d in (1, 2, 3):
-            ty_copy(j, d).wait_recv()
+        for h in range(4):
+            ty_copy(j, h).wait_recv()
 
         def total(x):
-            rows = pl.ds(pl.multiple_of(y * 256 + x * 128, 128), 128)
-            here = pl.ds(pl.multiple_of(x * 128, 128), 128)
-            result = terms[j, rows, :].astype(F32)
-            for d in range(3):
-                result = result + y_got[j, d, here, :].astype(F32)
-            return result
+            return (
+                terms[j, term_rows(y, x), :].astype(F32)
+                + y_got[j, x].astype(F32)
+                + y_got[j, 2 + x].astype(F32)
+            )
 
         x_send[j] = total(1 - x_lo).astype(BF16)
         tx_copy(j).start()
@@ -418,6 +433,7 @@
     send_heads(1)
     stage_terms(1)
     send_heads(2)
+    stage_second(0)
     dk_sum[...] = jnp.zeros_like(dk_sum)
     dv_sum[...] = jnp.zeros_like(dv_sum)
     dk_far[...] = jnp.zeros_like(dk_far)
@@ -428,38 +444,28 @@
         def _():
             stage_terms(j)
 
-        stage_ty(j - 2)
-
-        @pl.when(j >= 3)
-        def _():
-            stage_tx(j - 3)
-
-        return carry
-
-    lax.fori_loop(2, 8, way_in, 0)
-    stage_tx(5)
+        @pl.when((j >= 2) & (j <= 8))
+        def _():
+            stage_second(j - 1)
+
+        @pl.when((j >= 3) & (j < 11))
+        def _():
+            stage_ty(j - 3)
+
+        @pl.when(j >= 4)
+        def _():
+            stage_tx(j - 4)
+
+        return carry
+
+    lax.fori_loop(2, 12, way_in, 0)
     many = o_buf.at[pl.ds(0, 31 * ROWS)]
     for a in range(3):
         source, target = (q_ref, k_ref, v_ref)[a], (qh, kh, vh)[a]
         pltpu.make_async_copy(source.at[:, :, col(0)], target.at[pl.ds(0, 2)], own_sem.at[a]).wait()
         pltpu.make_async_copy(many, many, recv_sem.at[a]).wait()
 
-    def forward_part(part, carry):
-        lax.fori_loop(part * 4, part * 4 + 4, forward_pair, 0)
-
-        @pl.when(part == 0)
-        def _():
-            stage_ty(6)
-
-        @pl.when(part == 1)
-        def _():
-            stage_tx(6)
-
-        return carry
-
-    lax.fori_loop(0, 4, forward_part, 0)
-    stage_ty(7)
-    stage_tx(7)
+    lax.fori_loop(0, 16, forward_pair, 0)
     pltpu.make_async_copy(g_send.at[0, :, 0:HD], gh.at[row(0), :], own_sem.at[3]).wait()
     pltpu.make_async_copy(many, many, g_recv_sem).wait()
 
@@ -481,8 +487,8 @@
     stage_neighbour(near_far(NZ - 1, z, NZ))
 
     def drain_in(j, carry):
-        for d in (1, 2, 3):
-            ty_copy(j, d).wait_send()
+        for h in range(6):
+            ty_copy(j, h).wait_send()
         tx_copy(j).wait_send()
         return carry
 
@@ -554,7 +560,7 @@
             pltpu.VMEM((8 * ROWS, WIDE), BF16),
             pltpu.VMEM((D, WIDE), BF16),
             pltpu.VMEM((8, 8 * ROWS, WIDE), BF16),
-            pltpu.VMEM((8, 3, 256, WIDE), BF16),
+            pltpu.VMEM((8, 6, ROWS, WIDE), BF16),
             pltpu.VMEM((8, ROWS, WIDE), F32),
             piece, piece, piece,
             tiles, tiles, tiles, head, head, head, head, head,
@@ -564,7 +570,7 @@
             pltpu.VMEM((NZ, 2 * ROWS, WIDE), BF16),
             piece, piece,
             pltpu.VMEM((ROWS, WIDE), F32),
-            dma((2,)), dma((4,)), dma((3,)), dma((3,)), dma((8, 3)), dma((8, 3)), dma((8,)), dma((8,)),
+            dma((2,)), dma((4,)), dma((3,)), dma((3,)), dma((8, 6)), dma((8, 6)), dma((8,)), dma((8,)),
             dma, dma,
             dma, dma((NZ,)), dma((3,)), dma((3,)), dma((3,)), dma,
             dma((NZ,)), dma((NZ,)), dma((2, 2, NZ)), dma((2, 2, NZ)), dma((2, NZ)), dma((2, NZ)),

time: 250 us -> 238 us (0.952)
  Pallas kernels: 236 us -> 225 us
    pallas_call x1, Pallas kernels: 236 us -> 225 us  [whole(): pl.pallas_call(whole_kernel, out_shape=[tokens] * 4 + [jax.ShapeDtypeStru...]
where the time goes in v3:
time: 238 us; the launch traced here: 234 us
  Pallas kernels  225 us (95%)
  local copies, waits for them, and re-layouts  8.15 us (3%)
    pallas_call x1, Pallas kernels, whole(): pl.pallas_call(whole_kernel, out_shape=[tokens] * 4 + [jax.ShapeDtypeStru...  225 us
    unnamed x11, local copies, waits for them, and re-layouts  7.38 us

profile of v3, /device:TPU:32, one launch (start us, length us, event | category | flops | bytes accessed | tf_op | source)
XLA Modules:
  0.0 234.4 jit_solution(10002949423027054126)
XLA Ops:
  0.6 0.7 slice_bitcast_fusion
  1.3 0.1 eq.34
  1.4 0.7 select_reduce_fusion.table_ref
  2.1 224.9 %whole.1 = (bf16[128,4096]{1,0:T(8,128)(2,1)}, bf16[128,4096]{1,0:T(8,128)(2,1)}, bf16[128,4096]{1,0:T(8,128)(2,1)}, bf16[128,4096]{1,0:T(8,128)(2,1)}, f32[128,512]{1,0:T(8,128)}) custom-call(s32[192]{0:T(256)} %select_reduce_fusion.table_ref, bf16[2,64,4096]{2,1,0:T(8,128)(2,1)} %bitcast.10, bf16[2,64,4096]{2,1,0:T(8,128)(2,1)} %bitcast.11, ...), custom_call_target="tpu_custom_call" | custom-call | tf_op jit(solution)/shard_map/whole/pallas_call | solution.py:554
  227.0 0.0 copy-start.1
  227.0 0.0 copy-start
  227.0 0.0 copy-start.2
  227.0 2.4 %copy.16 = bf16[1,128,4096]{2,1,0:T(8,128)(2,1)} copy(bf16[1,128,4096]{2,1,0:T(8,128)(2,1)} %bitcast.17) | data formatting | bytes 2097152
  229.5 2.3 copy.17
  231.7 0.0 copy-done.1
  231.7 1.0 copy.18
  232.7 0.0 copy-done
  232.7 1.0 copy.19
  233.7 0.0 copy-done.2
  233.7 0.7 copy.20
  (5 shorter events, 0.0 us)
Async XLA Ops:
  227.0 4.8 %copy-start.1 = (bf16[128,4096]{1,0:T(8,128)(2,1)S(1)}, bf16[128,4096]{1,0:T(8,128)(2,1)}, u32[]{:S(2)}) copy-start(bf16[128,4096]{1,0:T(8,128)(2,1)} %get-tuple-element.12) | copy-start | bytes 3145732
  227.0 5.7 %copy-start = (bf16[128,4096]{1,0:T(8,128)(2,1)S(1)}, bf16[128,4096]{1,0:T(8,128)(2,1)}, u32[]{:S(2)}) copy-start(bf16[128,4096]{1,0:T(8,128)(2,1)} %get-tuple-element.13) | copy-start | bytes 3145732
  227.0 6.7 %copy-start.2 = (f32[128,512]{1,0:T(8,128)S(1)}, f32[128,512]{1,0:T(8,128)}, u32[]{:S(2)}) copy-start(f32[128,512]{1,0:T(8,128)} %get-tuple-element.30) | copy-start | bytes 786436

commit v4 on v3

--- a/solution.py
+++ b/solution.py
@@ -81,7 +81,7 @@
     att_ref, dqt_ref, dkt_ref, dvt_ref, gw_ref,
     u_buf, w_buf, terms, y_got, keep, x_send, x_got, g_send,
     qh, kh, vh, gh, o_buf, dq_buf, dk_buf, dv_buf, soft_buf, dk_sum, dv_sum, dk_far, dv_far,
-    every, c_got, xh_got, z_got, final,
+    every, c_got, xh_got, z_got,
     load_sem, own_sem, send_sem, recv_sem, ty_send_sem, ty_recv_sem, tx_send_sem, tx_recv_sem,
     g_send_sem, g_recv_sem,
     a_send_sem, a_recv_sem, d_own_sem, d_send_sem, d_recv_sem, att_sem,
@@ -203,8 +203,11 @@
                     device_id_type=MESH,
                 ).start()
 
+    def visit(i):
+        return seq_peer(NSEQ - 1 - i, me)
+
     def block_at(n):
-        return 2 * seq_peer(n // 2, me) + lax.rem(n, 2)
+        return 2 * visit(n // 2) + lax.rem(n, 2)
 
     def tile(a):
         return pl.ds(pl.multiple_of(a * BLK, BLK), BLK)
@@ -216,13 +219,13 @@
         return jnp.concatenate([ref[b] for b in window(a) + (table_ref[a],)], axis=0)
 
     def send_rows(source, target, sem_send, sem_recv, sem_own, i):
-        peer = seq_peer(i, me)
-
-        @pl.when(i == 0)
+        peer = visit(i)
+
+        @pl.when(i == NSEQ - 1)
         def _():
             pltpu.make_async_copy(source.at[row(me), :], target, sem_own).start()
 
-        @pl.when(i > 0)
+        @pl.when(i < NSEQ - 1)
         def _():
             pltpu.make_async_remote_copy(
                 src_ref=source.at[row(peer), :],
@@ -287,7 +290,7 @@
 
     def finish_keys(i, carry):
         for m in range(2):
-            b = 2 * seq_peer(i, me) + m
+            b = 2 * visit(i) + m
             dk_buf[tile(b), :] = (dk_sum[tile(b), :] + dk_far[table_ref[128 + b]]).astype(BF16)
             dv_buf[tile(b), :] = (dv_sum[tile(b), :] + dv_far[table_ref[128 + b]]).astype(BF16)
         for n, (source, target) in enumerate(((dk_buf, dkt_ref), (dv_buf, dvt_ref))):
@@ -356,15 +359,25 @@
             device_id_type=MESH,
         )
 
+    def steps_up(chunk):
+        return lax.rem(chunk + NZ - z, NZ)
+
     def z_copy(chunk):
+        t = steps_up(chunk)
+        goes_up = (t < 4) | ((t == 4) & (core == 0))
+        target = lax.rem(jnp.where(goes_up, z + 1, z + NZ - 1), NZ)
+        slot = jnp.where((target == chunk) & jnp.logical_not(goes_up), NZ, chunk)
         return pltpu.make_async_remote_copy(
             src_ref=g_send.at[chunk],
-            dst_ref=z_got.at[z],
+            dst_ref=z_got.at[slot],
             send_sem=z_send_sem.at[chunk],
-            recv_sem=z_recv_sem,
-            device_id=(seq_of(x_hi, chunk, core), tp),
+            recv_sem=z_recv_sem.at[slot],
+            device_id=(seq_of(x_hi, target, core), tp),
             device_id_type=MESH,
         )
+
+    def z_wait(slot):
+        pltpu.make_async_copy(z_got.at[slot], z_got.at[slot], z_recv_sem.at[slot]).wait()
 
     def stage_attended(chunk):
         here = every.at[chunk, row(tp), :]
@@ -410,21 +423,33 @@
 
     def stage_xh(chunk):
         xh_copy(chunk).wait_recv()
-        total = keep[chunk] + xh_got[chunk].astype(F32)
-
-        @pl.when(chunk == z)
-        def _():
-            final[...] = total
-
-        @pl.when(chunk != z)
-        def _():
-            g_send[chunk] = total.astype(BF16)
+        t = steps_up(chunk)
+        more = (
+            (t == 1) | (t == 2) | (t == 6) | (t == 7)
+            | ((t == 3) & (core == 0)) | ((t == 5) & (core == 1))
+        )
+        keep[chunk] += xh_got[chunk].astype(F32)
+
+        @pl.when(t == 0)
+        def _():
+            z_wait(chunk)
+            z_wait(NZ)
+            gw_ref[...] = keep[chunk] + z_got[chunk].astype(F32) + z_got[NZ].astype(F32)
+
+        @pl.when(more)
+        def _():
+            z_wait(chunk)
+            keep[chunk] += z_got[chunk].astype(F32)
+
+        @pl.when(t != 0)
+        def _():
+            g_send[chunk] = keep[chunk].astype(BF16)
             z_copy(chunk).start()
 
     def when_in(s, low, high, stage):
         @pl.when((s >= low) & (s < high))
         def _():
-            stage(near_far(s, z, NZ))
+            stage(chunk_at(s, z))
 
     send_heads(0)
     load_u.wait()
@@ -475,7 +500,7 @@
         @pl.when(lax.rem(i, 2) == 1)
         def _():
             s = i // 2
-            stage_attended(near_far(s, z, NZ))
+            stage_attended(chunk_at(s, z))
             when_in(s - 1, 0, NZ, stage_neighbour)
             when_in(s - 5, 0, NZ, stage_relay)
 
@@ -484,7 +509,7 @@
     lax.fori_loop(0, 16, backward_part, 0)
     lax.fori_loop(0, D // BLK, link_far, 0)
     lax.fori_loop(0, NSEQ, finish_keys, 0)
-    stage_neighbour(near_far(NZ - 1, z, NZ))
+    stage_neighbour(chunk_at(NZ - 1, z))
 
     def drain_in(j, carry):
         for h in range(6):
@@ -522,15 +547,6 @@
         return carry
 
     lax.fori_loop(0, NZ, drain_out, 0)
-    seven = z_got.at[pl.ds(0, NZ - 1)]
-    pltpu.make_async_copy(seven, seven, z_recv_sem).wait()
-
-    def add(d, carry):
-        final[...] += z_got[lax.rem(z + d, NZ)].astype(F32)
-        return carry
-
-    lax.fori_loop(1, NZ, add, 0)
-    gw_ref[...] = final[...]
     whole = every.at[0, row(0), :]
     for chunk in range(NZ):
         pltpu.make_async_copy(whole, whole, att_sem).wait()
@@ -568,13 +584,12 @@
             head_sum, head_sum, far_sum, far_sum,
             pltpu.VMEM((NZ, 8 * ROWS, WIDE), BF16),
             pltpu.VMEM((NZ, 2 * ROWS, WIDE), BF16),
-            piece, piece,
-            pltpu.VMEM((ROWS, WIDE), F32),
+            piece, pltpu.VMEM((NZ + 1, ROWS, WIDE), BF16),
             dma((2,)), dma((4,)), dma((3,)), dma((3,)), dma((8, 6)), dma((8, 6)), dma((8,)), dma((8,)),
             dma, dma,
             dma, dma((NZ,)), dma((3,)), dma((3,)), dma((3,)), dma,
             dma((NZ,)), dma((NZ,)), dma((2, 2, NZ)), dma((2, 2, NZ)), dma((2, NZ)), dma((2, NZ)),
-            dma((NZ,)), dma((NZ,)), dma((NZ,)), dma((NZ,)), dma((NZ,)), dma,
+            dma((NZ,)), dma((NZ,)), dma((NZ,)), dma((NZ,)), dma((NZ,)), dma((NZ + 1,)),
         ],
         compiler_params=pltpu.CompilerParams(
             collective_id=0, has_side_effects=True, vmem_limit_bytes=63 << 20

time: 238 us -> 235 us (0.987)
  no operation moved by 1% of the time
where the time goes in v4:
time: 235 us; the launch traced here: 233 us
  Pallas kernels  223 us (95%)
  local copies, waits for them, and re-layouts  8.15 us (3%)
    pallas_call x1, Pallas kernels, whole(): pl.pallas_call(whole_kernel, out_shape=[tokens] * 4 + [jax.ShapeDtypeStru...  223 us
    unnamed x11, local copies, waits for them, and re-layouts  7.38 us

profile of v4, /device:TPU:32, one launch (start us, length us, event | category | flops | bytes accessed | tf_op | source)
XLA Modules:
  0.0 232.7 jit_solution(2089368407623808975)
XLA Ops:
  0.6 0.7 slice_bitcast_fusion
  1.3 0.1 eq.34
  1.4 0.7 select_reduce_fusion.table_ref
  2.1 223.2 %whole.1 = (bf16[128,4096]{1,0:T(8,128)(2,1)}, bf16[128,4096]{1,0:T(8,128)(2,1)}, bf16[128,4096]{1,0:T(8,128)(2,1)}, bf16[128,4096]{1,0:T(8,128)(2,1)}, f32[128,512]{1,0:T(8,128)}) custom-call(s32[192]{0:T(256)} %select_reduce_fusion.table_ref, bf16[2,64,4096]{2,1,0:T(8,128)(2,1)} %bitcast.10, bf16[2,64,4096]{2,1,0:T(8,128)(2,1)} %bitcast.11, ...), custom_call_target="tpu_custom_call" | custom-call | tf_op jit(solution)/shard_map/whole/pallas_call | solution.py:570
  225.3 0.0 copy-start.1
  225.3 0.0 copy-start
  225.3 0.0 copy-start.2
  225.3 2.4 %copy.16 = bf16[1,128,4096]{2,1,0:T(8,128)(2,1)} copy(bf16[1,128,4096]{2,1,0:T(8,128)(2,1)} %bitcast.17) | data formatting | bytes 2097152
  227.8 2.3 copy.17
  230.1 0.0 copy-done.1
  230.1 1.0 copy.18
  231.0 0.0 copy-done
  231.0 1.0 copy.19
  232.0 0.0 copy-done.2
  232.0 0.7 copy.20
  (5 shorter events, 0.0 us)
Async XLA Ops:
  225.3 4.8 %copy-start.1 = (bf16[128,4096]{1,0:T(8,128)(2,1)S(1)}, bf16[128,4096]{1,0:T(8,128)(2,1)}, u32[]{:S(2)}) copy-start(bf16[128,4096]{1,0:T(8,128)(2,1)} %get-tuple-element.12) | copy-start | bytes 3145732
  225.3 5.7 %copy-start = (bf16[128,4096]{1,0:T(8,128)(2,1)S(1)}, bf16[128,4096]{1,0:T(8,128)(2,1)}, u32[]{:S(2)}) copy-start(bf16[128,4096]{1,0:T(8,128)(2,1)} %get-tuple-element.13) | copy-start | bytes 3145732
  225.3 6.7 %copy-start.2 = (f32[128,512]{1,0:T(8,128)S(1)}, f32[128,512]{1,0:T(8,128)}, u32[]{:S(2)}) copy-start(f32[128,512]{1,0:T(8,128)} %get-tuple-element.30) | copy-start | bytes 786436
